TPU v7x, 256 devices: a whole 4x4x8 slice. The times are simulated.
256 devices in a mesh: grp: 8 (over z), tok: 32 (over y, x, core).
Axes of the slice: x: 4, y: 4, z: 8, core: 2. Of those that a mesh axis runs over, the one named last changes fastest.
Arguments:
- residual_in: bfloat16 [8192, 2048], P(('tok', 'grp')), may hold values from -2.5 to 2.5
- queries: bfloat16 [8192, 2048], P('tok', 'grp'), may hold values from -120 to 120
- fresh_pairs: bfloat16 [8192, 2048], P('tok'), may hold values from -6 to 6
- cache_pairs: bfloat16 [16384, 2048], P('tok'), may hold values from -6 to 6
- segment_ids: int32 [8192], replicated, may hold values from 0 to 15, never falling along the last dimension, each value on 1 to 4096 neighbouring positions
- prefix_length: int32 [16], replicated, may hold values from 0 to 256, as said below
- page_order: int32 [1024], replicated, may hold values from 0 to 1023, each once
- out_weight: bfloat16 [2048, 2048], P('grp'), may hold values from -0.125 to 0.125
- post_gain: float32 [2048], replicated, may hold values from 0.25 to 1.75
- gate_weight: bfloat16 [2048, 4096], P(None, 'grp'), may hold values from -0.125 to 0.125
- up_weight: bfloat16 [2048, 4096], P(None, 'grp'), may hold values from -0.125 to 0.125
- down_weight: bfloat16 [4096, 2048], P('grp'), may hold values from -0.09375 to 0.09375
- next_gain: float32 [2048], replicated, may hold values from 0.25 to 1.75
- next_weight: bfloat16 [2048, 4096], P(None, 'grp'), may hold values from -0.125 to 0.125
Outputs:
- attended: bfloat16 [8192, 2048], P('tok', 'grp')
- new_cache: bfloat16 [16384, 2048], P('tok', 'grp')
- layer_out: bfloat16 [8192, 2048], P(('tok', 'grp'))
- next_proj: bfloat16 [8192, 4096], P('tok', 'grp')
Inputs may be any that keep to these rules, and one draw needn't show every extreme that they name: `segment_ids`: segment numbers never fall along the stream; each of the 16 segments has 1 to 4096 tokens and one has exactly 4096. `prefix_length`: one segment has exactly 256 cached tokens. `page_order`: each page number appears once.
All inputs are finite; a program needn't handle non-finite values.
Results may differ from a plain program's by a relative error of at most 0.024.
Values may be sent and summed in bfloat16 or wider, within the bound.
A program may use at most 128 MiB of HBM per device.

v0:
```python
import math

import jax
import jax.numpy as jnp
from jax import lax
from jax.sharding import PartitionSpec as P

HD = 256
PAGE = 16


masked_score = -1e30
norm_epsilon = 1e-05


def page_tables(segment_ids, prefix_length, page_order, page_rows):
    seg_count = prefix_length.shape[0]
    seg_range = jnp.arange(seg_count, dtype=jnp.int32)
    seg_len = jnp.sum(
        (segment_ids[None, :] == seg_range[:, None]).astype(jnp.int32), axis=1, dtype=jnp.int32
    )
    seg_start = jnp.cumsum(seg_len, dtype=jnp.int32) - seg_len
    needed = (prefix_length + seg_len + page_rows - 1) // page_rows
    cum_end = jnp.cumsum(needed, dtype=jnp.int32)
    first_slot = cum_end - needed
    page_count = page_order.shape[0]
    page_range = jnp.arange(page_count, dtype=jnp.int32)
    ranking = jnp.sum(
        jnp.where(page_order[None, :] == page_range[:, None], page_range[None, :], 0),
        axis=1,
        dtype=jnp.int32,
    )
    owners = jnp.sum(
        (cum_end[None, :] <= ranking[:, None]).astype(jnp.int32), axis=1, dtype=jnp.int32
    )
    onehot = (owners[:, None] == seg_range[None, :]).astype(jnp.int32)
    page_first = (
        ranking - jnp.sum(onehot * first_slot[None, :], axis=1, dtype=jnp.int32)
    ) * page_rows
    page_prefix = jnp.sum(onehot * prefix_length[None, :], axis=1, dtype=jnp.int32)
    page_len = jnp.sum(onehot * seg_len[None, :], axis=1, dtype=jnp.int32)
    page_start = jnp.sum(onehot * seg_start[None, :], axis=1, dtype=jnp.int32)
    return (owners, page_first, page_prefix, page_len, page_start)


def row_info(tables, row_first, count, page_rows):
    sliced = [
        jnp.repeat(
            lax.dynamic_slice_in_dim(table, row_first // page_rows, count // page_rows), page_rows
        )
        for table in tables
    ]
    position = sliced[1] + (row_first + jnp.arange(count, dtype=jnp.int32)) % page_rows
    return (sliced[0], position, sliced[2], sliced[3], sliced[4])


def attend_piece(state, query_four, pairs, visible):
    maxima, totals, weighted = state
    rows_here = pairs.shape[0]
    split = pairs.reshape(rows_here, query_four.shape[1], 2, query_four.shape[3])
    score_scale = 1.0 / math.sqrt(HD)
    scores = (
        jnp.einsum("tkgd,nkd->tkgn", query_four, split[:, :, 0], preferred_element_type=jnp.float32)
        * score_scale
    )
    live = visible[:, None, None, :]
    scores = jnp.where(live, scores, masked_score)
    raised = jnp.maximum(maxima, jnp.max(scores, axis=3))
    weights = jnp.where(live, jnp.exp(scores - raised[..., None]), 0.0)
    rescale = jnp.exp(maxima - raised)
    totals = totals * rescale + jnp.sum(weights, axis=3)
    weighted = weighted * rescale[..., None] + jnp.einsum(
        "tkgn,nkd->tkgd",
        weights.astype(jnp.bfloat16),
        split[:, :, 1],
        preferred_element_type=jnp.float32,
    )
    return (raised, totals, weighted)


def update_state(state, query_four, pairs, visible):
    return attend_piece(state, query_four, pairs, visible)


def empty_state(rows_here, pairs_here, per_pair):
    return (
        jnp.full((rows_here, pairs_here, per_pair), masked_score, jnp.float32),
        jnp.zeros((rows_here, pairs_here, per_pair), jnp.float32),
        jnp.zeros((rows_here, pairs_here, per_pair, HD), jnp.float32),
    )


def rms_scale(rows, gain):
    values = rows.astype(jnp.float32)
    scaled = values * lax.rsqrt(jnp.mean(values * values, axis=-1, keepdims=True) + norm_epsilon)
    return (scaled * gain).astype(jnp.bfloat16)


def local(
    residual_in,
    queries,
    fresh_pairs,
    cache_pairs,
    segment_ids,
    prefix_length,
    page_order,
    out_weight,
    post_gain,
    gate_weight,
    up_weight,
    down_weight,
    next_gain,
    next_weight,
):
    group = lax.axis_index("grp")
    shard = lax.axis_index("tok")
    groups = lax.axis_size("grp")
    tok_rows = queries.shape[0]
    heads_here = queries.shape[1] // HD
    pairs_here = max(1, heads_here // 2)
    per_pair = heads_here // pairs_here
    kv_first = group * heads_here // 2
    width_pairs = pairs_here * 2 * HD
    own_cols = cache_pairs.shape[1] // groups
    own_offset = group * own_cols - kv_first * 2 * HD
    query_four = queries.reshape(tok_rows, pairs_here, per_pair, HD)
    own_first = shard * tok_rows
    own_pos = own_first + jnp.arange(tok_rows, dtype=jnp.int32)
    own_seg = lax.dynamic_slice_in_dim(segment_ids, own_first, tok_rows)
    tables = page_tables(segment_ids, prefix_length, page_order, PAGE)
    cache_rows = cache_pairs.shape[0]
    cache_first = shard * cache_rows
    fresh_mine = lax.dynamic_slice_in_dim(fresh_pairs, kv_first * 2 * HD, width_pairs, 1)
    cache_mine = lax.dynamic_slice_in_dim(cache_pairs, kv_first * 2 * HD, width_pairs, 1)
    cache_info = row_info(tables, cache_first, cache_rows, PAGE)
    portion = lax.all_gather(cache_mine, "tok", axis=0, tiled=True)
    info = row_info(tables, jnp.int32(0), portion.shape[0], PAGE)
    visible = (info[0][None, :] == own_seg[:, None]) & (info[1] < info[2])[None, :]
    state = update_state(empty_state(tok_rows, pairs_here, per_pair), query_four, portion, visible)
    write_live = (cache_info[1] >= cache_info[2]) & (cache_info[1] < cache_info[2] + cache_info[3])
    write_token = cache_info[4] + cache_info[1] - cache_info[2]
    own_cache = lax.dynamic_slice_in_dim(cache_pairs, group * own_cols, own_cols, 1)
    portion = lax.all_gather(fresh_mine, "tok", axis=0, tiled=True)
    current = state
    written = own_cache
    count = portion.shape[0]
    key_pos = jnp.arange(count, dtype=jnp.int32)
    visible = (segment_ids[None, :] == own_seg[:, None]) & (key_pos[None, :] <= own_pos[:, None])
    current = update_state(current, query_four, portion, visible)
    landing = write_live & (write_token >= 0) & (write_token < count)
    mine = lax.dynamic_slice_in_dim(portion, own_offset, own_cols, 1)
    taken = jnp.take(mine, jnp.clip(write_token, 0, count - 1), axis=0)
    written = jnp.where(landing[:, None], taken, written)
    maxima, totals, weighted = current
    attended = (
        (weighted / totals[..., None]).reshape(tok_rows, heads_here * HD).astype(jnp.bfloat16)
    )
    mixed = lax.psum_scatter(
        jnp.dot(attended, out_weight, preferred_element_type=jnp.float32).astype(jnp.bfloat16),
        "grp",
        scatter_dimension=0,
        tiled=True,
    ).astype(jnp.float32)
    first_sum = (residual_in.astype(jnp.float32) + mixed).astype(jnp.bfloat16)
    post_normed = rms_scale(first_sum, post_gain)
    portion = lax.all_gather(post_normed, "grp", axis=0, tiled=True)
    gate = jnp.dot(portion, gate_weight, preferred_element_type=jnp.float32)
    up_part = jnp.dot(portion, up_weight, preferred_element_type=jnp.float32)
    hidden = (jax.nn.silu(gate) * up_part).astype(jnp.bfloat16)
    partial_rows = jnp.dot(hidden, down_weight, preferred_element_type=jnp.float32)
    ffn_out = lax.psum_scatter(
        partial_rows.astype(jnp.bfloat16), "grp", scatter_dimension=0, tiled=True
    ).astype(jnp.float32)
    layer_out = (first_sum.astype(jnp.float32) + ffn_out).astype(jnp.bfloat16)
    next_normed = rms_scale(layer_out, next_gain)
    next_proj = jnp.dot(
        lax.all_gather(next_normed, "grp", axis=0, tiled=True),
        next_weight,
        preferred_element_type=jnp.float32,
    ).astype(jnp.bfloat16)
    return (attended, written, layer_out, next_proj)


def solution(mesh):
    in_specs = (
        P(("tok", "grp"), None),
        P("tok", "grp"),
        P("tok", None),
        P("tok", None),
        P(),
        P(),
        P(),
        P("grp", None),
        P(),
        P(None, "grp"),
        P(None, "grp"),
        P("grp", None),
        P(),
        P(None, "grp"),
    )
    out_specs = (P("tok", "grp"), P("tok", "grp"), P(("tok", "grp"), None), P("tok", "grp"))
    return jax.shard_map(local, mesh=mesh, in_specs=in_specs, out_specs=out_specs, check_vma=False)
```

profile of v0, /device:TPU:30, one launch (start us, length us, event | category | flops | bytes accessed | tf_op | source)
XLA Modules:
  0.0 376.7 jit_solution(1616883388557246644)
XLA Ops:
  7.2 1.8 constant_dynamic-slice_fusion.1
  9.1 1.1 constant_dynamic-slice_fusion.2
  10.2 1.0 copy.42
  11.3 0.8 dynamic_slice.30
  12.1 0.9 convert_reduce_fusion
  14.2 1.2 select_reduce_fusion
  15.5 1.4 select_reduce_fusion.2
  18.1 51.5 %all-gather.7.cloned.1.call-done = bf16[8192,512]{1,0:T(8,128)(2,1)} async-done(((bf16[256,512]{1,0:T(8,128)(2,1)}), bf16[8192,512]{1,0:T(8,128)(2,1)}) %all-gather.7.cloned.1.call-update) | async-done | bytes 8388624 | tf_op jit(solution)/shard_map/all_gather | solution.py:143
  69.7 12.5 %reshape.514 = bf16[8192,1,2,256]{3,2,0,1:T(2,128)(2,1)} reshape(bf16[8192,512]{1,0:T(8,128)(2,1)} %all-gather.7.cloned.1.call-done) | data formatting | bytes 16777216 | tf_op jit(solution)/shard_map/reshape | solution.py:60
  82.2 17.2 %fusion.78 = (bf16[8192,1,1,256]{3,2,0,1:T(2,128)(2,1)}, bf16[8192,1,1,256]{3,2,0,1:T(2,128)(2,1)S(1)}) fusion(bf16[8192,1,2,256]{3,2,0,1:T(2,128)(2,1)} %reshape.514), kind=kLoop, calls=%fused_computation.121 | loop fusion | bytes 16777216 | tf_op jit(solution)/shard_map/slice | solution.py:75
  99.4 7.7 %fusion.81 = (f32[256]{0:T(256)S(1)}, f32[256,1,1,8192]{0,3,2,1:T(8,128)}) fusion(bf16[256,256]{1,0:T(8,128)(2,1)S(1)} %copy-done.9, bf16[8192,1,1,256]{3,2,0,1:T(2,128)(2,1)S(1)} %get-tuple-element.29, s32[256]{0:T(256)S(1)} %iota_add_fusion, s32[256]{0:T(256)S(1)} %dynamic_slice.30, s32[8192]{0:T(1024)S(1)} %copy-done.6), kind=kOutput, calls=%fused_computation.124 | convolution fusion | flops 1086324480 | bytes 12749824 | tf_op jit(solution)/shard_map/tkgd,nkd->tkgn/dot_general | solution.py:63
  107.1 50.1 %all-gather.5.cloned.1.call-done = bf16[16384,512]{0,1:T(8,128)(2,1)} async-done(((bf16[512,512]{0,1:T(8,128)(2,1)}), bf16[16384,512]{0,1:T(8,128)(2,1)}) %all-gather.5.cloned.1.call-update) | async-done | bytes 16777232 | tf_op jit(solution)/shard_map/all_gather | solution.py:136
  157.2 9.8 %fusion.80 = (f32[256]{0:T(256)S(1)}, f32[256,1,1,16384]{0,3,2,1:T(8,128)S(1)}) fusion(bf16[256,256]{1,0:T(8,128)(2,1)S(1)} %copy-done.9, bf16[16384,1,2,256]{0,3,2,1:T(8,128)(2,1)} %bitcast.108, pred[16384]{0:T(1024)(128)(4,1)S(1)} %fusion.62, s32[256]{0:T(256)S(1)} %dynamic_slice.30, s32[16384]{0:T(1024)S(1)} %eq.89), kind=kOutput, calls=%fused_computation.123 | convolution fusion | flops 2168454912 | bytes 25380864 | tf_op jit(solution)/shard_map/tkgd,nkd->tkgn/dot_general | solution.py:63
  167.0 3.9 %fusion.14 = f32[256]{0:T(256)S(1)} fusion(f32[256,1,1,8192]{0,3,2,1:T(8,128)S(1)} %copy-done.1, f32[256]{0:T(256)S(1)} %get-tuple-element.33, s32[256]{0:T(256)S(1)} %iota_add_fusion, s32[256]{0:T(256)S(1)} %dynamic_slice.30, s32[8192]{0:T(1024)S(1)} %copy-done.6), kind=kLoop, calls=%fused_computation.22 | loop fusion | flops 12582656 | bytes 8425472 | tf_op jit(solution)/shard_map/reduce_sum | solution.py:71
  170.9 3.2 fusion.24
  174.1 6.0 %fusion.2 = f32[256]{0:T(256)S(1)} fusion(f32[256,1,1,16384]{0,3,2,1:T(8,128)S(1)} %get-tuple-element.38, f32[256]{0:T(256)S(1)} %get-tuple-element.34, s32[256]{0:T(256)S(1)} %dynamic_slice.30, s32[16384]{0:T(1024)S(1)} %eq.89, pred[16384]{0:T(1024)(128)(4,1)S(1)} %fusion.62), kind=kLoop, calls=%fused_computation.6 | loop fusion | flops 20971264 | bytes 16862208 | tf_op jit(solution)/shard_map/reduce_sum | solution.py:71
  180.2 20.1 %fusion.45 = bf16[256,256]{0,1:T(8,128)(2,1)S(1)} fusion(f32[1,256,256,1]{2,1,3,0:T(8,128)S(1)} %fusion.24, f32[256,1,1,16384]{0,3,2,1:T(8,128)S(1)} %get-tuple-element.38, f32[256]{0:T(256)S(1)} %get-tuple-element.34, s32[256]{0:T(256)S(1)} %dynamic_slice.30, s32[16384]{0:T(1024)S(1)} %eq.89, pred[16384]{0:T(1024)(128)(4,1)S(1)} %fusion.62, ...), kind=kOutput, calls=%fused_computation.46 | convolution fusion | flops 2168782848 | bytes 25646080 | tf_op jit(solution)/shard_map/tkgn,nkd->tkgd/dot_general | solution.py:72
  200.3 1.5 convolution_convert_fusion.1
  201.8 40.8 %reduce-scatter.3.cloned.1.call-done = bf16[32,2048]{1,0:T(8,128)(2,1)} async-done(((bf16[256,2048]{1,0:T(8,128)(2,1)}), bf16[32,2048]{1,0:T(8,128)(2,1)}) %reduce-scatter.3.cloned.1.call-update) | async-done | bytes 131088 | tf_op jit(solution)/shard_map/reduce_scatter | solution.py:158
  242.6 1.1 fusion.56
  243.8 1.7 fusion.58
  245.7 37.0 %all-gather.9.cloned.1.call-done = bf16[256,2048]{1,0:T(8,128)(2,1)} async-done(((bf16[32,2048]{1,0:T(8,128)(2,1)}), bf16[256,2048]{1,0:T(8,128)(2,1)}) %all-gather.9.cloned.1.call-update) | async-done | bytes 1048592 | tf_op jit(solution)/shard_map/all_gather | solution.py:166
  282.7 2.6 fusion.82
  285.3 4.3 %convolution_convert_fusion = bf16[256,2048]{1,0:T(8,128)(2,1)} fusion(bf16[512,2048]{1,0:T(8,128)(2,1)S(1)} %copy-done, bf16[256,2048]{1,0:T(8,128)(2,1)} %all-gather.9.cloned.1.call-done, bf16[2048,512]{1,0:T(8,128)(2,1)} %param.24, f32[256,512]{1,0:T(8,128)S(1)} %fusion.82), kind=kOutput, calls=%fused_computation.34 | convolution fusion | flops 1075052544 | bytes 6815744 | tf_op jit(solution)/shard_map/dot_general | solution.py:170
  289.7 37.5 %reduce-scatter.5.cloned.1.call-done = bf16[32,2048]{1,0:T(8,128)(2,1)} async-done(((bf16[256,2048]{1,0:T(8,128)(2,1)}), bf16[32,2048]{1,0:T(8,128)(2,1)}) %reduce-scatter.5.cloned.1.call-update) | async-done | bytes 131088 | tf_op jit(solution)/shard_map/reduce_scatter | solution.py:171
  327.1 1.1 fusion.53
  330.3 4.4 %constant_dynamic-slice_fusion = bf16[8192,256]{1,0:T(8,128)(2,1)} fusion(bf16[8192,512]{1,0:T(8,128)(2,1)} %all-gather.7.cloned.1.call-done, s32[]{:T(128)S(6)} %select_n.127), kind=kLoop, calls=%fused_computation.111 | loop fusion | bytes 8388612 | tf_op jit(solution)/shard_map/dynamic_slice | solution.py:151
  334.7 4.3 %gather_fusion = bf16[512,256]{1,0:T(8,128)(2,1)S(1)} fusion(bf16[8192,256]{1,0:T(8,128)(2,1)} %constant_dynamic-slice_fusion, s32[1024]{0:T(1024)S(1)} %pad_clamp_fusion), kind=kCustom, calls=%fused_computation | custom fusion | bytes 526336 | tf_op jit(solution)/shard_map/jit(_take)/gather | solution.py:152
  339.0 1.9 dynamic-slice_select_fusion
  340.9 0.8 copy.41
  341.6 24.9 %all-gather.11.cloned.1.call-done = bf16[256,2048]{1,0:T(8,128)(2,1)} async-done(((bf16[32,2048]{1,0:T(8,128)(2,1)}), bf16[256,2048]{1,0:T(8,128)(2,1)}) %all-gather.11.cloned.1.call-update) | async-done | bytes 1048592 | tf_op jit(solution)/shard_map/all_gather | solution.py:177
  366.5 3.3 convolution_convert_fusion.2
  (78 shorter events, 5.0 us)
Async XLA Ops:
  7.2 278.1 %copy-start = (bf16[512,2048]{1,0:T(8,128)(2,1)S(1)}, bf16[512,2048]{1,0:T(8,128)(2,1)}, u32[]{:S(2)}) copy-start(bf16[512,2048]{1,0:T(8,128)(2,1)} %param.25) | copy-start | bytes 6291460
  7.2 62.5 %all-gather.7.cloned.1.call-start = ((), (), s32[]{:S(2)}) async-start(), calls=%async_computation.3 | async-start | bytes 8650752 | tf_op jit(solution)/shard_map/all_gather | solution.py:143
  9.1 148.1 %all-gather.5.cloned.1.call-start = ((), (), s32[]{:S(2)}) async-start(), calls=%async_computation.2 | async-start | bytes 17301504 | tf_op jit(solution)/shard_map/all_gather | solution.py:136
  11.3 231.4 %reduce-scatter.3.cloned.1.call-start = ((), (), s32[]{:S(2)}) async-start(), calls=%async_computation.4 | async-start | bytes 1179648 | tf_op jit(solution)/shard_map/reduce_scatter | solution.py:158
  82.2 17.2 %copy-start.6 = (s32[8192]{0:T(1024)S(1)}, s32[8192]{0:T(1024)}, u32[]{:S(2)}) copy-start(s32[8192]{0:T(1024)} %param.18) | copy-start | bytes 98308
  82.2 17.2 %copy-start.9 = (bf16[256,256]{1,0:T(8,128)(2,1)S(1)}, bf16[256,256]{1,0:T(8,128)(2,1)}, u32[]{:S(2)}) copy-start(bf16[256,256]{1,0:T(8,128)(2,1)} %param.15) | copy-start | bytes 393220
  157.2 13.7 %slice-start = ((s8[8388608]{0:T(1024)(128)(4,1)}), s8[4194304]{0:T(1024)(128)(4,1)S(1)}, s32[]{:S(2)}) async-start(s8[8388608]{0:T(1024)(128)(4,1)} %bitcast.103), calls=%async_computation.8 | async-start | bytes 8388608
  157.2 9.8 %copy-start.1 = (f32[256,1,1,8192]{0,3,2,1:T(8,128)S(1)}, f32[256,1,1,8192]{0,3,2,1:T(8,128)}, u32[]{:S(2)}) copy-start(f32[256,1,1,8192]{0,3,2,1:T(8,128)} %get-tuple-element.40) | copy-start | bytes 25165828
  157.2 13.7 %slice-start.1 = ((s8[8388608]{0:T(1024)(128)(4,1)}), s8[4194304]{0:T(1024)(128)(4,1)S(1)}, s32[]{:S(2)}) async-start(s8[8388608]{0:T(1024)(128)(4,1)} %bitcast.103), calls=%async_computation.9 | async-start | bytes 8388608
  180.1 20.1 %copy-start.4 = (bf16[256,2048]{1,0:T(8,128)(2,1)S(1)}, bf16[256,2048]{1,0:T(8,128)(2,1)}, u32[]{:S(2)}) copy-start(bf16[256,2048]{1,0:T(8,128)(2,1)} %param.21) | copy-start | bytes 3145732
  180.1 62.5 %copy-start.2 = (bf16[32,2048]{1,0:T(8,128)(2,1)S(1)}, bf16[32,2048]{1,0:T(8,128)(2,1)}, u32[]{:S(2)}) copy-start(bf16[32,2048]{1,0:T(8,128)(2,1)} %param.14) | copy-start | bytes 393220
  180.1 63.6 %copy-start.7 = (f32[2048]{0:T(1024)S(1)}, f32[2048]{0:T(1024)}, u32[]{:S(2)}) copy-start(f32[2048]{0:T(1024)} %param.22) | copy-start | bytes 24580
  201.7 126.5 %copy-start.8 = (f32[2048]{0:T(1024)S(1)}, f32[2048]{0:T(1024)}, u32[]{:S(2)}) copy-start(f32[2048]{0:T(1024)} %param.26) | copy-start | bytes 24580
  201.8 80.9 %all-gather.9.cloned.1.call-start = ((), (), s32[]{:S(2)}) async-start(), calls=%async_computation.5 | async-start | bytes 1179648 | tf_op jit(solution)/shard_map/all_gather | solution.py:166
  242.6 84.5 %copy-start.3 = (bf16[32,2048]{1,0:T(8,128)(2,1)S(1)}, bf16[32,2048]{1,0:T(8,128)(2,1)}, u32[]{:S(2)}) copy-start(bf16[32,2048]{1,0:T(8,128)(2,1)} %reduce-scatter.3.cloned.1.call-done) | copy-start | bytes 393220
  245.5 81.7 %reduce-scatter.5.cloned.1.call-start = ((), (), s32[]{:S(2)}) async-start(), calls=%async_computation.6 | async-start | bytes 1179648 | tf_op jit(solution)/shard_map/reduce_scatter | solution.py:171
  289.6 76.9 %all-gather.11.cloned.1.call-start = ((), (), s32[]{:S(2)}) async-start(), calls=%async_computation.7 | async-start | bytes 1179648 | tf_op jit(solution)/shard_map/all_gather | solution.py:177
  328.2 41.6 %copy-start.5 = (bf16[32,2048]{1,0:T(8,128)(2,1)}, bf16[32,2048]{1,0:T(8,128)(2,1)S(1)}, u32[]{:S(2)}) copy-start(bf16[32,2048]{1,0:T(8,128)(2,1)S(1)} %get-tuple-element.25) | copy-start | bytes 393220
Sparse Core Ops, SparseCore 0:
  11.1 58.4 all-gather.6
  72.1 85.0 all-gather.4
  201.9 40.7 reduce-scatter.2
  245.6 37.0 all-gather.8
  289.7 37.3 reduce-scatter.4
  329.4 37.1 all-gather.10
where the time goes:
time: 378 us; the launch traced here: 377 us
  waiting for transfers between devices  242 us (64%)
  matrix products  52.4 us (14%)
  local copies, waits for them, and re-layouts  46.4 us (12%)
  other arithmetic  21.1 us (6%)
  between operations  14.5 us (4%)
    all_gather x1, waiting for transfers between devices, local(): portion = lax.all_gather(fresh_mine, 'tok', axis=0, tiled=True)  51.5 us
    all_gather x1, waiting for transfers between devices, local(): portion = lax.all_gather(cache_mine, 'tok', axis=0, tiled=True)  50.1 us
    reduce_scatter x1, waiting for transfers between devices, local(): lax.psum_scatter(jnp.dot(attended, out_weight, preferred_element_type=jnp...  40.8 us
    reduce_scatter x1, waiting for transfers between devices, local(): lax.psum_scatter(partial_rows.astype(jnp.bfloat16), 'grp', scatter_dimens...  37.5 us
    all_gather x1, waiting for transfers between devices, local(): portion = lax.all_gather(post_normed, 'grp', axis=0, tiled=True)  37 us
    all_gather x1, waiting for transfers between devices, local(): lax.all_gather(next_normed, 'grp', axis=0, tiled=True)  24.9 us
    dot_general x2, matrix products, attend_piece(): jnp.einsum('tkgn,nkd->tkgd', weights.astype(jnp.bfloat16), split[:, :, 1]...  23.3 us
    dot_general x2, matrix products, attend_piece(): jnp.einsum('tkgd,nkd->tkgn', query_four, split[:, :, 0], preferred_elemen...  17.5 us
  transfers between devices with their start and end apart: 6, of which 6 were waited for; matrix products, arithmetic and copies ran while one was open for 16% of the time, Pallas kernels for 0%

commit v1 on v0

v1 whole, which is shorter than its diff:
```python
import functools
import math

import jax
import jax.numpy as jnp
from jax import lax
from jax.experimental import pallas as pl
from jax.experimental.pallas import tpu as pltpu
from jax.sharding import PartitionSpec as P

HD = 256
PAGE = 16
TILE = 256
MESH = pl.DeviceIdType.MESH
VMEM_LIMIT = 60 * 1024 * 1024

masked_score = -1e30
norm_epsilon = 1e-05


def page_tables(segment_ids, prefix_length, page_order, page_rows):
    seg_count = prefix_length.shape[0]
    seg_range = jnp.arange(seg_count, dtype=jnp.int32)
    seg_len = jnp.sum(
        (segment_ids[None, :] == seg_range[:, None]).astype(jnp.int32), axis=1, dtype=jnp.int32
    )
    seg_start = jnp.cumsum(seg_len, dtype=jnp.int32) - seg_len
    needed = (prefix_length + seg_len + page_rows - 1) // page_rows
    cum_end = jnp.cumsum(needed, dtype=jnp.int32)
    first_slot = cum_end - needed
    page_count = page_order.shape[0]
    page_range = jnp.arange(page_count, dtype=jnp.int32)
    ranking = jnp.sum(
        jnp.where(page_order[None, :] == page_range[:, None], page_range[None, :], 0),
        axis=1,
        dtype=jnp.int32,
    )
    owners = jnp.sum(
        (cum_end[None, :] <= ranking[:, None]).astype(jnp.int32), axis=1, dtype=jnp.int32
    )
    onehot = (owners[:, None] == seg_range[None, :]).astype(jnp.int32)
    page_first = (
        ranking - jnp.sum(onehot * first_slot[None, :], axis=1, dtype=jnp.int32)
    ) * page_rows
    page_prefix = jnp.sum(onehot * prefix_length[None, :], axis=1, dtype=jnp.int32)
    page_len = jnp.sum(onehot * seg_len[None, :], axis=1, dtype=jnp.int32)
    page_start = jnp.sum(onehot * seg_start[None, :], axis=1, dtype=jnp.int32)
    return seg_start, first_slot, (owners, page_first, page_prefix, page_len, page_start)


def row_info(tables, row_first, count, page_rows):
    sliced = [
        jnp.repeat(
            lax.dynamic_slice_in_dim(table, row_first // page_rows, count // page_rows), page_rows
        )
        for table in tables
    ]
    position = sliced[1] + (row_first + jnp.arange(count, dtype=jnp.int32)) % page_rows
    return (sliced[0], position, sliced[2], sliced[3], sliced[4])


def attend_kernel(
    pages_per_seg,
    info_ref,
    prefix_ref,
    rows_ref,
    q_ref,
    seg_ref,
    low_ref,
    fresh_ref,
    cache_ref,
    out_ref,
    tiles,
    prefix_tile,
    peak,
    total,
    acc,
    tile_sem,
    page_sem,
):
    first, last, seg_lo, seg_hi = info_ref[0], info_ref[1], info_ref[2], info_ref[3]
    rows = q_ref.shape[0]

    def tile_copy(index, slot):
        source = fresh_ref.at[pl.ds(pl.multiple_of(index * TILE, TILE), TILE), :]
        return pltpu.make_async_copy(source, tiles.at[slot], tile_sem.at[slot])

    def page_copy(seg, j):
        row = pl.multiple_of(rows_ref[seg * pages_per_seg + j], PAGE)
        source = cache_ref.at[pl.ds(row, PAGE), :]
        return pltpu.make_async_copy(
            source, prefix_tile.at[pl.ds(pl.multiple_of(j * PAGE, PAGE), PAGE), :], page_sem.at[j]
        )

    def pages_of(seg):
        return (prefix_ref[seg] + PAGE - 1) // PAGE

    tile_copy(first, 0).start()
    prefix_tile[...] = jnp.zeros_like(prefix_tile)
    peak[...] = jnp.full_like(peak, masked_score)
    total[...] = jnp.zeros_like(total)
    acc[...] = jnp.zeros_like(acc)
    row_at = last * TILE + lax.broadcasted_iota(jnp.int32, (rows, TILE), 0)
    column = lax.broadcasted_iota(jnp.int32, (rows, TILE), 1)
    scale = 1.0 / math.sqrt(HD)

    def absorb(keys, values, live):
        scores = lax.dot_general(
            q_ref[...], keys, (((1,), (1,)), ((), ())), preferred_element_type=jnp.float32
        )
        scores = jnp.where(live, scores * scale, masked_score)
        before = peak[...]
        raised = jnp.maximum(before, jnp.max(scores, axis=1, keepdims=True))
        weights = jnp.where(live, jnp.exp(scores - raised), 0.0)
        rescale = jnp.exp(before - raised)
        peak[...] = raised
        total[...] = total[...] * rescale + jnp.sum(weights, axis=1, keepdims=True)
        acc[...] = acc[...] * rescale + jnp.dot(
            weights.astype(jnp.bfloat16), values, preferred_element_type=jnp.float32
        )

    @pl.loop(first, last + 1)
    def _(index):
        slot = (index - first) % 2
        tile_copy(index, slot).wait()

        @pl.when(index < last)
        def _():
            tile_copy(index + 1, 1 - slot).start()

        key_at = index * TILE + column
        live = (key_at >= low_ref[...]) & (key_at <= row_at)
        absorb(tiles[slot, :, :HD], tiles[slot, :, HD:], live)

    @pl.loop(seg_lo, seg_hi + 1)
    def _(seg):
        count = pages_of(seg)

        @pl.loop(0, count)
        def _(j):
            page_copy(seg, j).start()

        @pl.loop(0, count)
        def _(j):
            page_copy(seg, j).wait()

        @pl.when(count > 0)
        def _():
            live = (seg_ref[...] == seg) & (column < prefix_ref[seg])
            absorb(prefix_tile[:, :HD], prefix_tile[:, HD:], live)

    out_ref[...] = (acc[...] / total[...]).astype(out_ref.dtype)


def attend(info, prefix_length, page_rows, queries, own_seg, own_low, fresh, cache):
    rows = queries.shape[0]
    pages_per_seg = page_rows.shape[0] // prefix_length.shape[0]
    smem = pl.BlockSpec(memory_space=pltpu.SMEM)
    vmem = pl.BlockSpec(memory_space=pltpu.VMEM)
    hbm = pl.BlockSpec(memory_space=pl.ANY)
    return pl.pallas_call(
        functools.partial(attend_kernel, pages_per_seg),
        out_shape=jax.ShapeDtypeStruct((rows, HD), jnp.bfloat16),
        in_specs=[smem, smem, smem, vmem, vmem, vmem, hbm, hbm],
        out_specs=vmem,
        scratch_shapes=[
            pltpu.VMEM((2, TILE, 2 * HD), jnp.bfloat16),
            pltpu.VMEM((pages_per_seg * PAGE, 2 * HD), jnp.bfloat16),
            pltpu.VMEM((rows, 1), jnp.float32),
            pltpu.VMEM((rows, 1), jnp.float32),
            pltpu.VMEM((rows, HD), jnp.float32),
            pltpu.SemaphoreType.DMA((2,)),
            pltpu.SemaphoreType.DMA((pages_per_seg,)),
        ],
        name="attend",
    )(info, prefix_length, page_rows, queries, own_seg, own_low, fresh, cache)


def chain_kernel(
    groups,
    attended_ref,
    residual_ref,
    post_gain_ref,
    next_gain_ref,
    wo_hbm,
    wg_hbm,
    wu_hbm,
    wd_hbm,
    wn_hbm,
    layer_ref,
    next_ref,
    wo,
    wg,
    wu,
    wd,
    wn,
    partial,
    hidden,
    sums,
    outgoing,
    incoming,
    gathered,
    weight_sem,
    sum_send,
    sum_recv,
    copy_send,
    copy_recv,
):
    me = lax.axis_index("grp")
    width = layer_ref.shape[1]
    chunk = layer_ref.shape[0]
    half = width // 2
    far = groups // 2
    steps = (1, -1)
    neighbour = [lax.rem(me + 1, groups), lax.rem(me + groups - 1, groups)]

    loads = []
    for i, (source, target) in enumerate(
        ((wo_hbm, wo), (wg_hbm, wg), (wu_hbm, wu), (wd_hbm, wd), (wn_hbm, wn))
    ):
        loads.append(pltpu.make_async_copy(source, target, weight_sem.at[i]))
        loads[i].start()

    barrier = pltpu.get_barrier_semaphore()
    for d in range(2):
        pl.semaphore_signal(
            barrier, inc=1, device_id={"grp": neighbour[d]}, device_id_type=MESH
        )
    pl.semaphore_wait(barrier, 2)

    def rows_of(owner):
        index = lax.rem(owner + 2 * groups, groups)
        return pl.ds(pl.multiple_of(index * chunk, chunk), chunk)

    def columns_of(h):
        return pl.ds(h * half, half)

    def sum_copy(phase, d, h, s):
        return pltpu.make_async_remote_copy(
            src_ref=outgoing.at[phase, d, h, s],
            dst_ref=incoming.at[phase, d, h, s],
            send_sem=sum_send.at[phase, d, h, s],
            recv_sem=sum_recv.at[phase, d, h, s],
            device_id={"grp": neighbour[d]},
            device_id_type=MESH,
        )

    def gather_copy(phase, d, h, k):
        block = gathered.at[phase, rows_of(me - steps[d] * k), columns_of(h)]
        return pltpu.make_async_remote_copy(
            src_ref=block,
            dst_ref=block,
            send_sem=copy_send.at[phase, d, h, k],
            recv_sem=copy_recv.at[phase, d, h, k],
            device_id={"grp": neighbour[d]},
            device_id_type=MESH,
        )

    def reduce_scatter(phase):
        for s in range(far):
            for h in range(2):
                for d in range(2):
                    first = 0 if h == d else 1
                    if s < first:
                        continue
                    owner = me + steps[d] * (far - s)
                    value = partial[rows_of(owner), columns_of(h)]
                    if s > first:
                        sum_copy(phase, d, h, s - 1).wait_recv()
                        value = value + incoming[phase, d, h, s - 1].astype(jnp.float32)
                    outgoing[phase, d, h, s] = value.astype(jnp.bfloat16)
                    sum_copy(phase, d, h, s).start()
        for h in range(2):
            value = partial[rows_of(me), columns_of(h)]
            for d in range(2):
                sum_copy(phase, d, h, far - 1).wait_recv()
                value = value + incoming[phase, d, h, far - 1].astype(jnp.float32)
            sums[:, columns_of(h)] = value
        for s in range(far):
            for h in range(2):
                for d in range(2):
                    if s >= (0 if h == d else 1):
                        sum_copy(phase, d, h, s).wait_send()

    def all_gather(phase):
        for k in range(far):
            for h in range(2):
                for d in range(2):
                    if k >= (far if h == d else far - 1):
                        continue
                    if k > 0:
                        gather_copy(phase, d, h, k - 1).wait_recv()
                    gather_copy(phase, d, h, k).start()
        for h in range(2):
            for d in range(2):
                gather_copy(phase, d, h, (far if h == d else far - 1) - 1).wait_recv()
        for k in range(far):
            for h in range(2):
                for d in range(2):
                    if k < (far if h == d else far - 1):
                        gather_copy(phase, d, h, k).wait_send()

    def normed(values, gain_ref):
        scaled = values * lax.rsqrt(
            jnp.mean(values * values, axis=-1, keepdims=True) + norm_epsilon
        )
        return (scaled * gain_ref[...]).astype(jnp.bfloat16)

    loads[0].wait()

    @pl.loop(0, width // 256)
    def _(j):
        columns = pl.ds(pl.multiple_of(j * 256, 256), 256)
        partial[:, columns] = jnp.dot(
            attended_ref[...], wo[:, columns], preferred_element_type=jnp.float32
        )

    reduce_scatter(0)
    first_sum = (residual_ref[...].astype(jnp.float32) + sums[...]).astype(jnp.bfloat16)
    layer_ref[...] = first_sum
    gathered[0, rows_of(me), :] = normed(first_sum.astype(jnp.float32), post_gain_ref)
    all_gather(0)

    loads[1].wait()
    loads[2].wait()

    @pl.loop(0, wg.shape[1] // 256)
    def _(j):
        columns = pl.ds(pl.multiple_of(j * 256, 256), 256)
        rows = gathered[0]
        gate = jnp.dot(rows, wg[:, columns], preferred_element_type=jnp.float32)
        up = jnp.dot(rows, wu[:, columns], preferred_element_type=jnp.float32)
        hidden[:, columns] = (jax.nn.silu(gate) * up).astype(jnp.bfloat16)

    loads[3].wait()

    @pl.loop(0, width // 256)
    def _(j):
        columns = pl.ds(pl.multiple_of(j * 256, 256), 256)
        partial[:, columns] = jnp.dot(
            hidden[...], wd[:, columns], preferred_element_type=jnp.float32
        )

    reduce_scatter(1)
    layer_out = (layer_ref[...].astype(jnp.float32) + sums[...]).astype(jnp.bfloat16)
    layer_ref[...] = layer_out
    gathered[1, rows_of(me), :] = normed(layer_out.astype(jnp.float32), next_gain_ref)
    all_gather(1)

    loads[4].wait()

    @pl.loop(0, wn.shape[1] // 256)
    def _(j):
        columns = pl.ds(pl.multiple_of(j * 256, 256), 256)
        next_ref[:, columns] = jnp.dot(
            gathered[1], wn[:, columns], preferred_element_type=jnp.float32
        ).astype(jnp.bfloat16)


def chain(attended, residual, post_gain, next_gain, wo, wg, wu, wd, wn, groups):
    rows = attended.shape[0]
    chunk, width = residual.shape
    far = groups // 2
    vmem = pl.BlockSpec(memory_space=pltpu.VMEM)
    hbm = pl.BlockSpec(memory_space=pl.ANY)
    messages = (2, 2, 2, far)
    return pl.pallas_call(
        functools.partial(chain_kernel, groups),
        out_shape=(
            jax.ShapeDtypeStruct((chunk, width), jnp.bfloat16),
            jax.ShapeDtypeStruct((rows, wn.shape[1]), jnp.bfloat16),
        ),
        in_specs=[vmem] * 4 + [hbm] * 5,
        out_specs=(vmem, vmem),
        scratch_shapes=[pltpu.VMEM(w.shape, w.dtype) for w in (wo, wg, wu, wd, wn)]
        + [
            pltpu.VMEM((rows, width), jnp.float32),
            pltpu.VMEM((rows, wg.shape[1]), jnp.bfloat16),
            pltpu.VMEM((chunk, width), jnp.float32),
            pltpu.VMEM(messages + (chunk, width // 2), jnp.bfloat16),
            pltpu.VMEM(messages + (chunk, width // 2), jnp.bfloat16),
            pltpu.VMEM((2, rows, width), jnp.bfloat16),
            pltpu.SemaphoreType.DMA((5,)),
            pltpu.SemaphoreType.DMA(messages),
            pltpu.SemaphoreType.DMA(messages),
            pltpu.SemaphoreType.DMA(messages),
            pltpu.SemaphoreType.DMA(messages),
        ],
        compiler_params=pltpu.CompilerParams(
            collective_id=1, has_side_effects=True, vmem_limit_bytes=VMEM_LIMIT
        ),
        name="chain",
    )(attended, residual, post_gain, next_gain, wo, wg, wu, wd, wn)


def local(
    residual_in,
    queries,
    fresh_pairs,
    cache_pairs,
    segment_ids,
    prefix_length,
    page_order,
    out_weight,
    post_gain,
    gate_weight,
    up_weight,
    down_weight,
    next_gain,
    next_weight,
):
    group = lax.axis_index("grp")
    shard = lax.axis_index("tok")
    groups = lax.axis_size("grp")
    tok_rows = queries.shape[0]
    kv_first = group // 2
    width_pairs = 2 * HD
    own_cols = cache_pairs.shape[1] // groups
    own_offset = group * own_cols - kv_first * width_pairs
    own_first = shard * tok_rows
    own_seg = lax.dynamic_slice_in_dim(segment_ids, own_first, tok_rows)
    seg_start, first_slot, tables = page_tables(segment_ids, prefix_length, page_order, PAGE)
    cache_rows = cache_pairs.shape[0]
    cache_first = shard * cache_rows
    fresh_mine = lax.dynamic_slice_in_dim(fresh_pairs, kv_first * width_pairs, width_pairs, 1)
    cache_mine = lax.dynamic_slice_in_dim(cache_pairs, kv_first * width_pairs, width_pairs, 1)
    fresh_all = lax.all_gather(fresh_mine, "tok", axis=0, tiled=True)
    cache_all = lax.all_gather(cache_mine, "tok", axis=0, tiled=True)

    seg_range = jnp.arange(prefix_length.shape[0], dtype=jnp.int32)
    own_low = jnp.sum(
        jnp.where(own_seg[:, None] == seg_range[None, :], seg_start[None, :], 0), axis=1
    )
    info = jnp.stack([own_low[0] // TILE, shard * tok_rows // TILE, own_seg[0], own_seg[-1]])
    most_pages = 256 // PAGE
    slots = jnp.clip(
        first_slot[:, None] + jnp.arange(most_pages, dtype=jnp.int32)[None, :],
        0,
        page_order.shape[0] - 1,
    )
    page_rows = (page_order[slots] * PAGE).reshape(-1)
    attended = attend(
        info,
        prefix_length,
        page_rows,
        queries,
        own_seg[:, None],
        own_low[:, None],
        fresh_all,
        cache_all,
    )

    cache_info = row_info(tables, cache_first, cache_rows, PAGE)
    write_live = (cache_info[1] >= cache_info[2]) & (cache_info[1] < cache_info[2] + cache_info[3])
    write_token = cache_info[4] + cache_info[1] - cache_info[2]
    own_cache = lax.dynamic_slice_in_dim(cache_pairs, group * own_cols, own_cols, 1)
    mine = lax.dynamic_slice_in_dim(fresh_all, own_offset, own_cols, 1)
    taken = jnp.take(mine, jnp.clip(write_token, 0, fresh_all.shape[0] - 1), axis=0)
    written = jnp.where(write_live[:, None], taken, own_cache)

    layer_out, next_proj = chain(
        attended,
        residual_in,
        post_gain[None, :],
        next_gain[None, :],
        out_weight,
        gate_weight,
        up_weight,
        down_weight,
        next_weight,
        groups,
    )
    return (attended, written, layer_out, next_proj)


def solution(mesh):
    in_specs = (
        P(("tok", "grp"), None),
        P("tok", "grp"),
        P("tok", None),
        P("tok", None),
        P(),
        P(),
        P(),
        P("grp", None),
        P(),
        P(None, "grp"),
        P(None, "grp"),
        P("grp", None),
        P(),
        P(None, "grp"),
    )
    out_specs = (P("tok", "grp"), P("tok", "grp"), P(("tok", "grp"), None), P("tok", "grp"))
    return jax.shard_map(local, mesh=mesh, in_specs=in_specs, out_specs=out_specs, check_vma=False)
```

time: 378 us -> 259 us (0.69)
  waiting for transfers between devices: 242 us -> 112 us
  Pallas kernels: 0 us -> 98.7 us
  matrix products: 52.4 us -> 0 us
  local copies, waits for them, and re-layouts: 46.4 us -> 22 us
  other arithmetic: 21.1 us -> 8.5 us
    pallas_call x0 -> x2, Pallas kernels: none -> 98.7 us  [the longest x1 79.4 us: chain(): pl.pallas_call(functools.partial(chain_kernel, groups), out_shape=(jax.Sh...]
    reduce_scatter x2 -> x0, waiting for transfers between devices: 78.3 us -> none  [the longest x1 40.8 us: local(): lax.psum_scatter(jnp.dot(attended, out_weight, preferred_element_type=jnp...]
    dot_general x8 -> x0, matrix products: 52.4 us -> none  [the longest x2 23.3 us: attend_piece(): jnp.einsum('tkgn,nkd->tkgd', weights.astype(jnp.bfloat16), split[:, :, 1]...]
    all_gather x4 -> x2, waiting for transfers between devices: 164 us -> 112 us  [the longest x1 69.2 us: local(): cache_all = lax.all_gather(cache_mine, 'tok', axis=0, tiled=True)]
    slice x1 -> x2, local copies, waits for them, and re-layouts: 17.2 us -> 1.1 us  [the longest x1 0.58 us: local(): own_seg[0]]
    reshape x1 -> x0, local copies, waits for them, and re-layouts: 12.5 us -> none  [attend_piece(): pairs.reshape(rows_here, query_four.shape[1], 2, query_four.shape[3])]
    reduce_sum x4 -> x1, other arithmetic: 12 us -> 0.09 us  [local(): jnp.sum(jnp.where(own_seg[:, None] == seg_range[None, :], seg_start[None,...]
  transfers between devices with their start and end apart: 6 -> 2, of which waited for: 6 -> 2; matrix products, arithmetic and copies ran while one was open for 16% -> 10% of each run, Pallas kernels for 0% -> 0%
where the time goes in v1:
time: 259 us; the launch traced here: 258 us
  waiting for transfers between devices  112 us (43%)
  Pallas kernels  98.7 us (38%)
  local copies, waits for them, and re-layouts  22 us (8%)
  between operations  16.8 us (6%)
  other arithmetic  8.5 us (3%)
    pallas_call x1, Pallas kernels, chain(): pl.pallas_call(functools.partial(chain_kernel, groups), out_shape=(jax.Sh...  79.4 us
    all_gather x1, waiting for transfers between devices, local(): cache_all = lax.all_gather(cache_mine, 'tok', axis=0, tiled=True)  69.2 us
    all_gather x1, waiting for transfers between devices, local(): fresh_all = lax.all_gather(fresh_mine, 'tok', axis=0, tiled=True)  42.9 us
    pallas_call x1, Pallas kernels, attend(): pl.pallas_call(functools.partial(attend_kernel, pages_per_seg), out_shape...  19.3 us
  transfers between devices with their start and end apart: 2, of which 2 were waited for; matrix products, arithmetic and copies ran while one was open for 10% of the time, Pallas kernels for 0%

profile of v1, /device:TPU:30, one launch (start us, length us, event | category | flops | bytes accessed | tf_op | source)
XLA Modules:
  0.0 258.3 jit_solution(16034252358241788330)
XLA Ops:
  7.3 1.1 copy-done
  8.4 0.7 constant_dynamic-slice_fusion.2
  9.2 1.9 constant_dynamic-slice_fusion.1
  11.1 0.9 convert_reduce_fusion
  12.1 0.1 copy.24
  12.2 0.1 reduce
  12.3 0.7 and_select_fusion.1
  13.0 0.1 copy.25
  13.1 0.1 reduce.1
  13.3 1.2 select_reduce_fusion
  14.4 0.1 convert_reduce_fusion.1
  14.5 0.8 select_reduce_fusion.2
  15.8 0.1 reshape.256
  16.2 0.1 reshape.253
  16.3 0.8 dynamic_slice.27
  17.0 0.1 select_reduce_fusion.5
  17.1 0.5 slice.9
  20.5 0.8 copy.27.low_ref
  21.3 0.8 copy.26.seg_ref
  22.3 1.4 gather_fusion
  23.7 0.6 fusion.6
  24.2 1.9 pad_add_fusion.info_ref
  26.2 0.5 broadcast_multiply_fusion.rows_ref
  26.7 42.9 %all-gather.3.cloned.1.call-done.fresh_ref = bf16[8192,512]{1,0:T(8,128)(2,1)} async-done(((bf16[256,512]{1,0:T(8,128)(2,1)}), bf16[8192,512]{1,0:T(8,128)(2,1)}) %all-gather.3.cloned.1.call-update) | async-done | bytes 8388624 | tf_op jit(solution)/shard_map/all_gather | solution.py:427
  69.7 4.4 %constant_dynamic-slice_fusion = bf16[8192,256]{1,0:T(8,128)(2,1)} fusion(bf16[8192,512]{1,0:T(8,128)(2,1)} %all-gather.3.cloned.1.call-done.fresh_ref, s32[]{:T(128)S(6)} %select_n.116), kind=kLoop, calls=%fused_computation.39 | loop fusion | bytes 8388612 | tf_op jit(solution)/shard_map/dynamic_slice | solution.py:457
  74.1 4.3 %gather_fusion.1 = bf16[512,256]{1,0:T(8,128)(2,1)S(1)} fusion(bf16[8192,256]{1,0:T(8,128)(2,1)} %constant_dynamic-slice_fusion, s32[1024]{0:T(1024)S(1)} %pad_clamp_fusion), kind=kCustom, calls=%fused_computation.1 | custom fusion | bytes 526336 | tf_op jit(solution)/shard_map/jit(_take)/gather | solution.py:458
  78.4 1.9 dynamic-slice_select_fusion
  80.3 69.2 %all-gather.5.cloned.1.call-done.cache_ref = bf16[16384,512]{1,0:T(8,128)(2,1)} async-done(((bf16[512,512]{1,0:T(8,128)(2,1)}), bf16[16384,512]{1,0:T(8,128)(2,1)}) %all-gather.5.cloned.1.call-update) | async-done | bytes 16777232 | tf_op jit(solution)/shard_map/all_gather | solution.py:428
  149.5 19.3 %attend.1.attended_ref = bf16[256,256]{1,0:T(8,128)(2,1)} custom-call(s32[4]{0:T(128)} %pad_add_fusion.info_ref, s32[16]{0:T(128)} %prefix_ref.1, s32[256]{0:T(256)} %broadcast_multiply_fusion.rows_ref, bf16[256,256]{1,0:T(8,128)(2,1)} %q_ref.1, s32[256,1]{1,0:T(8,128)} %copy.26.seg_ref, s32[256,1]{1,0:T(8,128)} %copy.27.low_ref, ...), custom_call_target="tpu_custom_call" | custom-call | tf_op jit(solution)/shard_map/attend/pallas_call | solution.py:161
  168.7 79.4 %chain.1 = (bf16[32,2048]{1,0:T(8,128)(2,1)}, bf16[256,512]{1,0:T(8,128)(2,1)}) custom-call(bf16[256,256]{1,0:T(8,128)(2,1)} %attend.1.attended_ref, bf16[32,2048]{1,0:T(8,128)(2,1)} %residual_ref.1, f32[1,2048]{1,0:T(1,128)} %bitcast.13, f32[1,2048]{1,0:T(1,128)} %bitcast.14, bf16[256,2048]{1,0:T(8,128)(2,1)} %wo_hbm.1, bf16[2048,512]{1,0:T(8,128)(2,1)} %wg_hbm.1, ...), custom_call_target="tpu_custom_call" | custom-call | tf_op jit(solution)/shard_map/chain/pallas_call | solution.py:367
  248.2 1.6 copy.30
  249.7 1.7 copy.31
  (30 shorter events, 1.4 us)
Async XLA Ops:
  7.2 1.2 copy-start
  7.2 15.1 %copy-start.1 = (s32[1024]{0:T(1024)S(1)}, s32[1024]{0:T(1024)}, u32[]{:S(2)}) copy-start(s32[1024]{0:T(1024)} %param.20) | copy-start | bytes 12292
  7.2 62.5 %all-gather.3.cloned.1.call-start = ((), (), s32[]{:S(2)}) async-start(), calls=%async_computation | async-start | bytes 8650752 | tf_op jit(solution)/shard_map/all_gather | solution.py:427
  9.1 140.3 %all-gather.5.cloned.1.call-start = ((), (), s32[]{:S(2)}) async-start(), calls=%async_computation.1 | async-start | bytes 17301504 | tf_op jit(solution)/shard_map/all_gather | solution.py:428
Sparse Core Ops, SparseCore 0:
  11.1 58.4 all-gather.2
  72.2 77.1 all-gather.4

commit v2 on v1

--- a/solution.py
+++ b/solution.py
@@ -13,105 +13,373 @@
 TILE = 256
 MESH = pl.DeviceIdType.MESH
 VMEM_LIMIT = 60 * 1024 * 1024
+FEW_PAGES = 12
 
 masked_score = -1e30
+lowest_peak = -1e20
 norm_epsilon = 1e-05
 
-
-def page_tables(segment_ids, prefix_length, page_order, page_rows):
-    seg_count = prefix_length.shape[0]
-    seg_range = jnp.arange(seg_count, dtype=jnp.int32)
-    seg_len = jnp.sum(
-        (segment_ids[None, :] == seg_range[:, None]).astype(jnp.int32), axis=1, dtype=jnp.int32
-    )
-    seg_start = jnp.cumsum(seg_len, dtype=jnp.int32) - seg_len
-    needed = (prefix_length + seg_len + page_rows - 1) // page_rows
-    cum_end = jnp.cumsum(needed, dtype=jnp.int32)
-    first_slot = cum_end - needed
-    page_count = page_order.shape[0]
-    page_range = jnp.arange(page_count, dtype=jnp.int32)
-    ranking = jnp.sum(
-        jnp.where(page_order[None, :] == page_range[:, None], page_range[None, :], 0),
-        axis=1,
-        dtype=jnp.int32,
-    )
-    owners = jnp.sum(
-        (cum_end[None, :] <= ranking[:, None]).astype(jnp.int32), axis=1, dtype=jnp.int32
-    )
-    onehot = (owners[:, None] == seg_range[None, :]).astype(jnp.int32)
-    page_first = (
-        ranking - jnp.sum(onehot * first_slot[None, :], axis=1, dtype=jnp.int32)
-    ) * page_rows
-    page_prefix = jnp.sum(onehot * prefix_length[None, :], axis=1, dtype=jnp.int32)
-    page_len = jnp.sum(onehot * seg_len[None, :], axis=1, dtype=jnp.int32)
-    page_start = jnp.sum(onehot * seg_start[None, :], axis=1, dtype=jnp.int32)
-    return seg_start, first_slot, (owners, page_first, page_prefix, page_len, page_start)
-
-
-def row_info(tables, row_first, count, page_rows):
-    sliced = [
-        jnp.repeat(
-            lax.dynamic_slice_in_dim(table, row_first // page_rows, count // page_rows), page_rows
-        )
-        for table in tables
-    ]
-    position = sliced[1] + (row_first + jnp.arange(count, dtype=jnp.int32)) % page_rows
-    return (sliced[0], position, sliced[2], sliced[3], sliced[4])
-
-
-def attend_kernel(
-    pages_per_seg,
-    info_ref,
+START, LENGTH, SLOT, WHERE, SLOTS, COUNTS, MOST, TABLES = 0, 16, 32, 64, 320, 384, 448, 512
+
+smem = pl.BlockSpec(memory_space=pltpu.SMEM)
+vmem = pl.BlockSpec(memory_space=pltpu.VMEM)
+hbm = pl.BlockSpec(memory_space=pl.ANY)
+
+
+def pack_kernel(
+    shards,
+    ids_ref,
+    order_block_ref,
     prefix_ref,
-    rows_ref,
-    q_ref,
-    seg_ref,
-    low_ref,
+    order_ref,
     fresh_ref,
     cache_ref,
+    key_tile,
+    value_tile,
+    tables,
+    tile_sem,
+    page_sem,
+):
+    shard, group = lax.axis_index("tok"), lax.axis_index("grp")
+    own_pages = order_ref.shape[0] // shards
+    seg_count = prefix_ref.shape[0]
+    pairs_at = (group // 2) * 2 * HD
+    targets = (key_tile, value_tile)
+
+    def columns(part):
+        return pl.ds(pl.multiple_of(pairs_at + part * HD, HD), HD)
+
+    def fresh_copy(part):
+        return pltpu.make_async_copy(
+            fresh_ref.at[:, columns(part)],
+            targets[part].at[pl.ds(0, TILE), :],
+            tile_sem.at[part],
+        )
+
+    def page_copy(page, rank, part):
+        return pltpu.make_async_copy(
+            cache_ref.at[pl.ds(pl.multiple_of(page * PAGE, PAGE), PAGE), columns(part)],
+            targets[part].at[pl.ds(pl.multiple_of(TILE + rank * PAGE, PAGE), PAGE), :],
+            page_sem.at[rank, part],
+        )
+
+    for part in range(2):
+        fresh_copy(part).start()
+
+    ids = ids_ref[...]
+    starts = [jnp.int32(0)]
+    for s in range(1, seg_count):
+        starts.append(jnp.sum((ids < s).astype(jnp.float32)).astype(jnp.int32))
+    starts.append(jnp.int32(ids_ref.shape[0] * ids_ref.shape[1]))
+    slot = jnp.int32(0)
+    for s in range(seg_count):
+        length = starts[s + 1] - starts[s]
+        tables[START + s] = starts[s]
+        tables[LENGTH + s] = length
+        tables[SLOT + s] = slot
+        slot = slot + (prefix_ref[s] + length + PAGE - 1) // PAGE
+    tables[SLOT + seg_count] = slot
+
+    for owner in range(shards):
+        tables[COUNTS + owner] = 0
+    tables[MOST] = 0
+
+    @pl.loop(0, seg_count)
+    def _(s):
+        first = tables[SLOT + s]
+
+        @pl.loop(0, (prefix_ref[s] + PAGE - 1) // PAGE)
+        def _(j):
+            page = order_ref[first + j]
+            owner = page // own_pages
+            rank = tables[COUNTS + owner]
+            tables[COUNTS + owner] = rank + 1
+            tables[MOST] = jnp.maximum(tables[MOST], rank + 1)
+            tables[WHERE + s * PAGE + j] = owner * own_pages + rank
+
+            @pl.when(owner == shard)
+            def _():
+                for part in range(2):
+                    page_copy(page - owner * own_pages, rank, part).start()
+
+    order = order_block_ref[...]
+    at = lax.broadcasted_iota(jnp.int32, order.shape, 0) * order.shape[1] + (
+        lax.broadcasted_iota(jnp.int32, order.shape, 1)
+    )
+    at = at.astype(jnp.float32)
+    for i in range(own_pages):
+        mine = order == shard * own_pages + i
+        tables[SLOTS + i] = jnp.sum(jnp.where(mine, at, 0.0)).astype(jnp.int32)
+
+    @pl.loop(0, tables[COUNTS + shard])
+    def _(rank):
+        for part in range(2):
+            page_copy(0, rank, part).wait()
+
+    for part in range(2):
+        fresh_copy(part).wait()
+
+
+def pack(segment_ids, prefix_length, page_order, fresh, cache, shards):
+    own_pages = page_order.shape[0] // shards
+    tile = jax.ShapeDtypeStruct((TILE + own_pages * PAGE, HD), jnp.bfloat16)
+    return pl.pallas_call(
+        functools.partial(pack_kernel, shards),
+        out_shape=(tile, tile, jax.ShapeDtypeStruct((TABLES,), jnp.int32)),
+        in_specs=[vmem, vmem, smem, smem, hbm, hbm],
+        out_specs=(vmem, vmem, smem),
+        scratch_shapes=[
+            pltpu.SemaphoreType.DMA((2,)),
+            pltpu.SemaphoreType.DMA((own_pages, 2)),
+        ],
+        name="pack",
+    )(
+        segment_ids.reshape(-1, 128),
+        page_order.reshape(-1, 128),
+        prefix_length,
+        page_order,
+        fresh,
+        cache,
+    )
+
+
+SIDE = 4
+ROUTES = {
+    (0, 0): ("p+", "p-", "q+", "q-", "core"),
+    (3, 0): ("q+", "q-", "p+", "core"),
+    (1, 0): ("q+", "q-", "core"),
+    (0, 3): ("q+", "core"),
+    (0, 1): ("core",),
+    (2, 0): ("q+", "q-", "core"),
+    (3, 3): ("q+", "core"),
+    (3, 1): ("core",),
+    (1, 3): ("core",),
+    (1, 1): ("q-", "core"),
+    (0, 2): ("core",),
+    (2, 3): ("core",),
+    (2, 1): ("q-", "core"),
+    (3, 2): ("core",),
+    (1, 2): ("core",),
+    (2, 2): ("core",),
+}
+MOVES = {"p+": (1, 0), "p-": (-1, 0), "q+": (0, 1), "q-": (0, -1), "core": (0, 0)}
+MESSAGES = [(tile, way) for tile, ways in ROUTES.items() for way in ways]
+
+
+def arrival(tile):
+    for index, (sent, way) in enumerate(MESSAGES):
+        move = MOVES[way]
+        if way != "core" and ((sent[0] - move[0]) % SIDE, (sent[1] - move[1]) % SIDE) == tile:
+            return index
+    return None
+
+
+def spread_kernel(rows, key_ref, value_ref, keys, values, own, send_sem, recv_sem, own_sem):
+    shard = lax.axis_index("tok")
+    core, x, y = shard % 2, (shard // 2) % SIDE, shard // (2 * SIDE)
+
+    def shard_at(dx, dy, c):
+        return (((y + dy + SIDE) % SIDE) * SIDE + (x + dx + SIDE) % SIDE) * 2 + c
+
+    def place(part, p, q, c):
+        return shard_at(p, q, c) if part == 0 else shard_at(q, p, c)
+
+    sources, targets = (key_ref, value_ref), (keys, values)
+
+    def message(part, index):
+        tile, way = MESSAGES[index]
+        move = MOVES[way]
+        target = place(part, move[0], move[1], 1 - core if way == "core" else core)
+        block = targets[part].at[place(part, tile[0], tile[1], core)]
+        source = sources[part].at[pl.ds(0, rows), :] if tile == (0, 0) else block
+        return pltpu.make_async_remote_copy(
+            src_ref=source,
+            dst_ref=block,
+            send_sem=send_sem.at[part, index],
+            recv_sem=recv_sem.at[part, index],
+            device_id={"tok": target},
+            device_id_type=MESH,
+        )
+
+    def fetch(part):
+        return pltpu.make_async_copy(
+            sources[part].at[pl.ds(0, rows), :], own.at[part], own_sem.at[part]
+        )
+
+    def store(part):
+        return pltpu.make_async_copy(own.at[part], targets[part].at[shard], own_sem.at[part])
+
+    barrier = pltpu.get_barrier_semaphore()
+    peers = [shard_at(1, 0, core), shard_at(-1, 0, core), shard_at(0, 1, core)]
+    peers += [shard_at(0, -1, core), shard_at(0, 0, 1 - core)]
+    for peer in peers:
+        pl.semaphore_signal(barrier, inc=1, device_id={"tok": peer}, device_id_type=MESH)
+    for part in range(2):
+        fetch(part).start()
+    pl.semaphore_wait(barrier, len(peers))
+
+    for tile in ROUTES:
+        sent = [i for i, (t, _) in enumerate(MESSAGES) if t == tile]
+        for part in range(2):
+            if tile != (0, 0):
+                message(part, arrival(tile)).wait_recv()
+            for i in sent:
+                message(part, i).start()
+    for part in range(2):
+        fetch(part).wait()
+        store(part).start()
+    for part in range(2):
+        store(part).wait()
+    for part in range(2):
+        for i, (_, way) in enumerate(MESSAGES):
+            if way == "core":
+                message(part, i).wait_recv()
+    for part in range(2):
+        for i in range(len(MESSAGES)):
+            message(part, i).wait_send()
+
+
+def spread(key_tile, value_tile, rows, shards, collective_id):
+    tiles = jax.ShapeDtypeStruct((shards, rows, HD), jnp.bfloat16)
+    return pl.pallas_call(
+        functools.partial(spread_kernel, rows),
+        out_shape=(tiles, tiles),
+        in_specs=[hbm, hbm],
+        out_specs=(hbm, hbm),
+        scratch_shapes=[
+            pltpu.VMEM((2, rows, HD), jnp.bfloat16),
+            pltpu.SemaphoreType.DMA((2, len(MESSAGES))),
+            pltpu.SemaphoreType.DMA((2, len(MESSAGES))),
+            pltpu.SemaphoreType.DMA((2,)),
+        ],
+        compiler_params=pltpu.CompilerParams(collective_id=collective_id, has_side_effects=True),
+        name="spread",
+    )(key_tile, value_tile)
+
+
+def attend_kernel(
+    seg_count,
+    tables,
+    prefix_ref,
+    q_ref,
+    keys_ref,
+    values_ref,
+    cache_ref,
     out_ref,
-    tiles,
-    prefix_tile,
+    written_ref,
+    key_tiles,
+    value_tiles,
+    prefix_keys,
+    prefix_values,
+    windows,
+    query,
     peak,
     total,
     acc,
     tile_sem,
     page_sem,
+    window_sem,
+    cache_sem,
 ):
-    first, last, seg_lo, seg_hi = info_ref[0], info_ref[1], info_ref[2], info_ref[3]
+    shard, group = lax.axis_index("tok"), lax.axis_index("grp")
     rows = q_ref.shape[0]
-
-    def tile_copy(index, slot):
-        source = fresh_ref.at[pl.ds(pl.multiple_of(index * TILE, TILE), TILE), :]
-        return pltpu.make_async_copy(source, tiles.at[slot], tile_sem.at[slot])
-
-    def page_copy(seg, j):
-        row = pl.multiple_of(rows_ref[seg * pages_per_seg + j], PAGE)
-        source = cache_ref.at[pl.ds(row, PAGE), :]
+    own_pages = written_ref.shape[0] // PAGE
+    shards = keys_ref.shape[0]
+    sources = (keys_ref, values_ref)
+    tiles = (key_tiles, value_tiles)
+    prefixes = (prefix_keys, prefix_values)
+    wide = 2 * TILE
+
+    def cache_copy():
+        columns = pl.ds(pl.multiple_of(group * HD, HD), HD)
+        return pltpu.make_async_copy(cache_ref.at[:, columns], written_ref, cache_sem)
+
+    def page_place(i):
+        slot = tables[SLOTS + i]
+        seg = jnp.int32(-1)
+        for s in range(seg_count):
+            seg = seg + (tables[SLOT + s] <= slot).astype(jnp.int32)
+        position = (slot - tables[SLOT + seg]) * PAGE
+        return seg, position, tables[START + seg] + position - prefix_ref[seg]
+
+    def window_copy(part, i, side, block):
+        block = jnp.clip(block, 0, shards * (TILE // PAGE) - 1)
+        tile, row = block // (TILE // PAGE), (block % (TILE // PAGE)) * PAGE
         return pltpu.make_async_copy(
-            source, prefix_tile.at[pl.ds(pl.multiple_of(j * PAGE, PAGE), PAGE), :], page_sem.at[j]
-        )
-
-    def pages_of(seg):
-        return (prefix_ref[seg] + PAGE - 1) // PAGE
-
-    tile_copy(first, 0).start()
-    prefix_tile[...] = jnp.zeros_like(prefix_tile)
-    peak[...] = jnp.full_like(peak, masked_score)
+            sources[part].at[tile, pl.ds(pl.multiple_of(row, PAGE), PAGE), :],
+            windows.at[i, pl.ds(side * PAGE, PAGE), :],
+            window_sem.at[i, side],
+        )
+
+    def tile_copy(index, slot, side, part):
+        return pltpu.make_async_copy(
+            sources[part].at[jnp.maximum(index, 0), pl.ds(0, TILE), :],
+            tiles[part].at[slot, pl.ds(side * TILE, TILE), :],
+            tile_sem.at[slot, side, part],
+        )
+
+    def page_copy(seg, j, part):
+        place = tables[WHERE + seg * PAGE + j]
+        row = TILE + (place % own_pages) * PAGE
+        return pltpu.make_async_copy(
+            sources[part].at[place // own_pages, pl.ds(pl.multiple_of(row, PAGE), PAGE), :],
+            prefixes[part].at[pl.ds(pl.multiple_of(j * PAGE, PAGE), PAGE), :],
+            page_sem.at[j, part],
+        )
+
+    first_row = shard * rows
+    seg_lo = jnp.int32(-1)
+    seg_hi = jnp.int32(-1)
+    for s in range(seg_count):
+        seg_lo = seg_lo + (tables[START + s] <= first_row).astype(jnp.int32)
+        seg_hi = seg_hi + (tables[START + s] <= first_row + rows - 1).astype(jnp.int32)
+    first_tile = tables[START + seg_lo] // TILE
+    last_low = tables[START + seg_hi]
+    steps = (shard - first_tile) // 2 + 1
+    base = shard + 1 - 2 * steps
+
+    def start_tiles(step):
+        for side in range(2):
+            for part in range(2):
+                tile_copy(base + 2 * step + side, step % 2, side, part).start()
+
+    start_tiles(0)
+    cache_copy().start()
+
+    @pl.loop(0, own_pages)
+    def _(i):
+        _, _, token = page_place(i)
+        block = (token + wide * PAGE) // PAGE - wide
+        for part in range(2):
+
+            @pl.when(group % 2 == part)
+            def _():
+                for side in range(2):
+                    window_copy(part, i, side, block + side).start()
+
+    for part in range(2):
+        prefixes[part][...] = jnp.zeros_like(prefixes[part])
+    peak[...] = jnp.full_like(peak, lowest_peak)
     total[...] = jnp.zeros_like(total)
     acc[...] = jnp.zeros_like(acc)
-    row_at = last * TILE + lax.broadcasted_iota(jnp.int32, (rows, TILE), 0)
-    column = lax.broadcasted_iota(jnp.int32, (rows, TILE), 1)
-    scale = 1.0 / math.sqrt(HD)
+    query[...] = (q_ref[...].astype(jnp.float32) * (1.0 / math.sqrt(HD))).astype(jnp.bfloat16)
+    row_at = first_row + lax.broadcasted_iota(jnp.int32, (rows, 1), 0)
+    low = jnp.zeros((rows, 1), jnp.int32)
+    seg_at = jnp.full((rows, 1), -1, jnp.int32)
+    for s in range(seg_count):
+        begun = row_at >= tables[START + s]
+        low = jnp.where(begun, tables[START + s], low)
+        seg_at = seg_at + begun.astype(jnp.int32)
 
     def absorb(keys, values, live):
         scores = lax.dot_general(
-            q_ref[...], keys, (((1,), (1,)), ((), ())), preferred_element_type=jnp.float32
-        )
-        scores = jnp.where(live, scores * scale, masked_score)
+            query[...], keys, (((1,), (1,)), ((), ())), preferred_element_type=jnp.float32
+        )
+        if live is not None:
+            scores = jnp.where(live, scores, masked_score)
         before = peak[...]
         raised = jnp.maximum(before, jnp.max(scores, axis=1, keepdims=True))
-        weights = jnp.where(live, jnp.exp(scores - raised), 0.0)
+        weights = jnp.exp(scores - raised)
         rescale = jnp.exp(before - raised)
         peak[...] = raised
         total[...] = total[...] * rescale + jnp.sum(weights, axis=1, keepdims=True)
@@ -119,61 +387,99 @@
             weights.astype(jnp.bfloat16), values, preferred_element_type=jnp.float32
         )
 
-    @pl.loop(first, last + 1)
-    def _(index):
-        slot = (index - first) % 2
-        tile_copy(index, slot).wait()
-
-        @pl.when(index < last)
+    @pl.loop(0, steps)
+    def _(step):
+        slot = step % 2
+        for side in range(2):
+            for part in range(2):
+                tile_copy(base + 2 * step + side, slot, side, part).wait()
+
+        @pl.when(step + 1 < steps)
         def _():
-            tile_copy(index + 1, 1 - slot).start()
-
-        key_at = index * TILE + column
-        live = (key_at >= low_ref[...]) & (key_at <= row_at)
-        absorb(tiles[slot, :, :HD], tiles[slot, :, HD:], live)
+            start_tiles(step + 1)
+
+        at = (base + 2 * step) * TILE
+        whole = (at >= last_low) & (step + 1 < steps)
+
+        @pl.when(whole)
+        def _():
+            absorb(key_tiles[slot], value_tiles[slot], None)
+
+        @pl.when(jnp.logical_not(whole))
+        def _():
+            key_at = at + lax.broadcasted_iota(jnp.int32, (rows, wide), 1)
+            absorb(key_tiles[slot], value_tiles[slot], (key_at >= low) & (key_at <= row_at))
 
     @pl.loop(seg_lo, seg_hi + 1)
     def _(seg):
-        count = pages_of(seg)
+        count = (prefix_ref[seg] + PAGE - 1) // PAGE
 
         @pl.loop(0, count)
         def _(j):
-            page_copy(seg, j).start()
+            for part in range(2):
+                page_copy(seg, j, part).start()
 
         @pl.loop(0, count)
         def _(j):
-            page_copy(seg, j).wait()
+            for part in range(2):
+                page_copy(seg, j, part).wait()
 
         @pl.when(count > 0)
         def _():
-            live = (seg_ref[...] == seg) & (column < prefix_ref[seg])
-            absorb(prefix_tile[:, :HD], prefix_tile[:, HD:], live)
+            at = lax.broadcasted_iota(jnp.int32, (rows, prefix_keys.shape[0]), 1)
+            absorb(prefix_keys[...], prefix_values[...], (seg_at == seg) & (at < prefix_ref[seg]))
 
     out_ref[...] = (acc[...] / total[...]).astype(out_ref.dtype)
 
-
-def attend(info, prefix_length, page_rows, queries, own_seg, own_low, fresh, cache):
+    cache_copy().wait()
+
+    @pl.loop(0, own_pages)
+    def _(i):
+        seg, position, token = page_place(i)
+        for side in range(2):
+            window_copy(0, i, side, 0).wait()
+        shift = (token + wide * PAGE) % PAGE
+        line = lax.broadcasted_iota(jnp.int32, (PAGE, 2 * PAGE), 0)
+        taken = lax.broadcasted_iota(jnp.int32, (PAGE, 2 * PAGE), 1)
+        picked = (taken == line + shift).astype(jnp.bfloat16)
+        fresh = jnp.dot(picked, windows[i], preferred_element_type=jnp.float32)
+        at = position + lax.broadcasted_iota(jnp.int32, (PAGE, HD), 0)
+        used = tables[SLOTS + i] < tables[SLOT + seg_count]
+        live = (at >= prefix_ref[seg]) & (at < prefix_ref[seg] + tables[LENGTH + seg]) & used
+        block = pl.ds(pl.multiple_of(i * PAGE, PAGE), PAGE)
+        held = written_ref[block, :].astype(jnp.float32)
+        written_ref[block, :] = jnp.where(live, fresh, held).astype(jnp.bfloat16)
+
+
+def attend(tables, prefix_length, queries, keys, values, cache):
     rows = queries.shape[0]
-    pages_per_seg = page_rows.shape[0] // prefix_length.shape[0]
-    smem = pl.BlockSpec(memory_space=pltpu.SMEM)
-    vmem = pl.BlockSpec(memory_space=pltpu.VMEM)
-    hbm = pl.BlockSpec(memory_space=pl.ANY)
+    most = 256
+    own_pages = cache.shape[0] // PAGE
     return pl.pallas_call(
-        functools.partial(attend_kernel, pages_per_seg),
-        out_shape=jax.ShapeDtypeStruct((rows, HD), jnp.bfloat16),
-        in_specs=[smem, smem, smem, vmem, vmem, vmem, hbm, hbm],
-        out_specs=vmem,
+        functools.partial(attend_kernel, prefix_length.shape[0]),
+        out_shape=(
+            jax.ShapeDtypeStruct((rows, HD), jnp.bfloat16),
+            jax.ShapeDtypeStruct((cache.shape[0], HD), jnp.bfloat16),
+        ),
+        in_specs=[smem, smem, vmem, hbm, hbm, hbm],
+        out_specs=(vmem, vmem),
         scratch_shapes=[
-            pltpu.VMEM((2, TILE, 2 * HD), jnp.bfloat16),
-            pltpu.VMEM((pages_per_seg * PAGE, 2 * HD), jnp.bfloat16),
+            pltpu.VMEM((2, 2 * TILE, HD), jnp.bfloat16),
+            pltpu.VMEM((2, 2 * TILE, HD), jnp.bfloat16),
+            pltpu.VMEM((most, HD), jnp.bfloat16),
+            pltpu.VMEM((most, HD), jnp.bfloat16),
+            pltpu.VMEM((own_pages, 2 * PAGE, HD), jnp.bfloat16),
+            pltpu.VMEM((rows, HD), jnp.bfloat16),
             pltpu.VMEM((rows, 1), jnp.float32),
             pltpu.VMEM((rows, 1), jnp.float32),
             pltpu.VMEM((rows, HD), jnp.float32),
-            pltpu.SemaphoreType.DMA((2,)),
-            pltpu.SemaphoreType.DMA((pages_per_seg,)),
+            pltpu.SemaphoreType.DMA((2, 2, 2)),
+            pltpu.SemaphoreType.DMA((most // PAGE, 2)),
+            pltpu.SemaphoreType.DMA((own_pages, 2)),
+            pltpu.SemaphoreType.DMA(()),
         ],
         name="attend",
-    )(info, prefix_length, page_rows, queries, own_seg, own_low, fresh, cache)
+    )(tables, prefix_length, queries, keys, values, cache)
 
 
 def chain_kernel(
@@ -409,55 +715,21 @@
     next_gain,
     next_weight,
 ):
-    group = lax.axis_index("grp")
-    shard = lax.axis_index("tok")
-    groups = lax.axis_size("grp")
-    tok_rows = queries.shape[0]
-    kv_first = group // 2
-    width_pairs = 2 * HD
-    own_cols = cache_pairs.shape[1] // groups
-    own_offset = group * own_cols - kv_first * width_pairs
-    own_first = shard * tok_rows
-    own_seg = lax.dynamic_slice_in_dim(segment_ids, own_first, tok_rows)
-    seg_start, first_slot, tables = page_tables(segment_ids, prefix_length, page_order, PAGE)
-    cache_rows = cache_pairs.shape[0]
-    cache_first = shard * cache_rows
-    fresh_mine = lax.dynamic_slice_in_dim(fresh_pairs, kv_first * width_pairs, width_pairs, 1)
-    cache_mine = lax.dynamic_slice_in_dim(cache_pairs, kv_first * width_pairs, width_pairs, 1)
-    fresh_all = lax.all_gather(fresh_mine, "tok", axis=0, tiled=True)
-    cache_all = lax.all_gather(cache_mine, "tok", axis=0, tiled=True)
-
-    seg_range = jnp.arange(prefix_length.shape[0], dtype=jnp.int32)
-    own_low = jnp.sum(
-        jnp.where(own_seg[:, None] == seg_range[None, :], seg_start[None, :], 0), axis=1
+    groups, shards = lax.axis_size("grp"), lax.axis_size("tok")
+    own_pages = page_order.shape[0] // shards
+    key_tile, value_tile, tables = pack(
+        segment_ids, prefix_length, page_order, fresh_pairs, cache_pairs, shards
     )
-    info = jnp.stack([own_low[0] // TILE, shard * tok_rows // TILE, own_seg[0], own_seg[-1]])
-    most_pages = 256 // PAGE
-    slots = jnp.clip(
-        first_slot[:, None] + jnp.arange(most_pages, dtype=jnp.int32)[None, :],
-        0,
-        page_order.shape[0] - 1,
+
+    def attention(pages, collective_id):
+        keys, values = spread(key_tile, value_tile, TILE + pages * PAGE, shards, collective_id)
+        return attend(tables, prefix_length, queries, keys, values, cache_pairs)
+
+    attended, written = lax.cond(
+        tables[MOST] <= FEW_PAGES,
+        lambda: attention(FEW_PAGES, 2),
+        lambda: attention(own_pages, 3),
     )
-    page_rows = (page_order[slots] * PAGE).reshape(-1)
-    attended = attend(
-        info,
-        prefix_length,
-        page_rows,
-        queries,
-        own_seg[:, None],
-        own_low[:, None],
-        fresh_all,
-        cache_all,
-    )
-
-    cache_info = row_info(tables, cache_first, cache_rows, PAGE)
-    write_live = (cache_info[1] >= cache_info[2]) & (cache_info[1] < cache_info[2] + cache_info[3])
-    write_token = cache_info[4] + cache_info[1] - cache_info[2]
-    own_cache = lax.dynamic_slice_in_dim(cache_pairs, group * own_cols, own_cols, 1)
-    mine = lax.dynamic_slice_in_dim(fresh_all, own_offset, own_cols, 1)
-    taken = jnp.take(mine, jnp.clip(write_token, 0, fresh_all.shape[0] - 1), axis=0)
-    written = jnp.where(write_live[:, None], taken, own_cache)
-
     layer_out, next_proj = chain(
         attended,
         residual_in,

time: 259 us -> 159 us (0.61)
  waiting for transfers between devices: 112 us -> 0 us
  Pallas kernels: 98.7 us -> 153 us
  local copies, waits for them, and re-layouts: 22 us -> 3.84 us
  between operations: 16.8 us -> 1.37 us
  other arithmetic: 8.5 us -> 0 us
    all_gather x2 -> x0, waiting for transfers between devices: 112 us -> none  [the longest x1 69.2 us: local(): cache_all = lax.all_gather(cache_mine, 'tok', axis=0, tiled=True)]
    pallas_call x1 -> x3, Pallas kernels: 19.3 us -> 75.4 us  [the longest x1 47.7 us: spread(): pl.pallas_call(functools.partial(spread_kernel, rows), out_shape=(tiles,...]
    dynamic_slice x8 -> x0, local copies, waits for them, and re-layouts: 8.14 us -> none  [the longest x1 4.43 us: local(): mine = lax.dynamic_slice_in_dim(fresh_all, own_offset, own_cols, 1)]
    gather x2 -> x0, local copies, waits for them, and re-layouts: 5.65 us -> none  [the longest x1 4.29 us: local(): jnp.take(mine, jnp.clip(write_token, 0, fresh_all.shape[0] - 1), axis=0)]
    reduce_sum x5 -> x0, other arithmetic: 3.07 us -> none  [the longest x1 1.19 us: page_tables(): jnp.sum(jnp.where(page_order[None, :] == page_range[:, None], page_range[...]
    select_n x4 -> x0, other arithmetic: 2.63 us -> none  [the longest x1 1.87 us: local(): written = jnp.where(write_live[:, None], taken, own_cache)]
  transfers between devices with their start and end apart: 2 -> 0, of which waited for: 2 -> 0; matrix products, arithmetic and copies ran while one was open for 10% -> 0% of each run, Pallas kernels for 0% -> 0%
where the time goes in v2:
time: 159 us; the launch traced here: 158 us
  Pallas kernels  153 us (96%)
  local copies, waits for them, and re-layouts  3.84 us (2%)
    pallas_call x1, Pallas kernels, chain(): pl.pallas_call(functools.partial(chain_kernel, groups), out_shape=(jax.Sh...  77.7 us
    pallas_call x1, Pallas kernels, spread(): pl.pallas_call(functools.partial(spread_kernel, rows), out_shape=(tiles,...  47.7 us
    pallas_call x1, Pallas kernels, attend(): pl.pallas_call(functools.partial(attend_kernel, prefix_length.shape[0]),...  21.7 us
    pallas_call x1, Pallas kernels, pack(): pl.pallas_call(functools.partial(pack_kernel, shards), out_shape=(tile, t...  5.97 us
    unnamed x10, local copies, waits for them, and re-layouts  3.26 us

profile of v2, /device:TPU:30, one launch (start us, length us, event | category | flops | bytes accessed | tf_op | source)
XLA Modules:
  0.0 158.3 jit_solution(16405431466964887122)
XLA Ops:
  0.6 0.0 copy-start.3
  0.6 0.0 copy-start
  0.7 0.0 copy-start.1
  0.7 6.0 %pack.1 = (bf16[768,256]{1,0:T(8,128)(2,1)S(1)}, bf16[768,256]{1,0:T(8,128)(2,1)S(1)}, s32[512]{0:T(512)S(1)}) custom-call(s32[64,128]{1,0:T(8,128)} %bitcast.5, s32[8,128]{1,0:T(8,128)} %bitcast.6, s32[16]{0:T(128)} %prefix_ref.1, s32[1024]{0:T(1024)} %order_ref.1, bf16[256,2048]{1,0:T(8,128)(2,1)} %fresh_ref.1, bf16[512,2048]{1,0:T(8,128)(2,1)} %cache_ref.1), custom_call_target="tpu_custom_call" | custom-call | tf_op jit(solution)/shard_map/pack/pallas_call | solution.py:126
  6.6 0.6 slice.3
  7.9 0.0 copy-done.3
  7.9 0.0 copy-done
  7.9 0.0 copy-done.1
  7.9 69.4 %conditional.1 = ((bf16[256,256]{1,0:T(8,128)(2,1)S(1)}, bf16[512,256]{1,0:T(8,128)(2,1)})) conditional(s32[]{:T(128)} %bitcast.2, (bf16[768,256]{1,0:T(8,128)(2,1)S(1)}, bf16[768,256]{1,0:T(8,128)(2,1)S(1)}, s32[512]{0:T(512)S(1)}, s32[16]{0:T(128)S(1)}, bf16[256,256]{1,0:T(8,128)(2,1)S(1)}, /*index=5*/bf16[512,2048]{1,0:T(8,128)(2,1)S(1)}) %tuple.26, ...), branch_computations={%region_0.0_spmd, %region_1.0_spmd} | conditional | bytes 8 | solution.py:728
  7.9 47.7 %spread.3 = (bf16[32,448,256]{2,1,0:T(8,128)(2,1)}, bf16[32,448,256]{2,1,0:T(8,128)(2,1)}) custom-call(bf16[768,256]{1,0:T(8,128)(2,1)S(1)} %get-tuple-element.35.key_ref, bf16[768,256]{1,0:T(8,128)(2,1)S(1)} %get-tuple-element.36.value_ref), custom_call_target="tpu_custom_call" | custom-call | tf_op jit(solution)/shard_map/cond/branch_1_fun/spread/pallas_call | solution.py:244
  55.7 21.7 %attend.3 = (bf16[256,256]{1,0:T(8,128)(2,1)S(1)}, bf16[512,256]{1,0:T(8,128)(2,1)}) custom-call(s32[512]{0:T(512)S(1)} %get-tuple-element.32.tables, s32[16]{0:T(128)S(1)} %get-tuple-element.33.prefix_ref, bf16[256,256]{1,0:T(8,128)(2,1)S(1)} %get-tuple-element.34.q_ref, bf16[32,448,256]{2,1,0:T(8,128)(2,1)} %get-tuple-element.37.keys_ref, ...), custom_call_target="tpu_custom_call" | custom-call | tf_op jit(solution)/shard_map/cond/branch_1_fun/attend/pallas_call | solution.py:458
  77.3 0.0 copy-start.2
  77.4 77.7 %chain.1 = (bf16[32,2048]{1,0:T(8,128)(2,1)}, bf16[256,512]{1,0:T(8,128)(2,1)}) custom-call(bf16[256,256]{1,0:T(8,128)(2,1)S(1)} %get-tuple-element.66.attended_ref, bf16[32,2048]{1,0:T(8,128)(2,1)} %residual_ref.1, f32[1,2048]{1,0:T(1,128)} %bitcast.7, f32[1,2048]{1,0:T(1,128)} %bitcast.8, bf16[256,2048]{1,0:T(8,128)(2,1)} %wo_hbm.1, ...), custom_call_target="tpu_custom_call" | custom-call | tf_op jit(solution)/shard_map/chain/pallas_call | solution.py:673
  155.1 0.0 copy-done.2
  155.1 1.6 copy.24
  156.6 1.7 %copy.25 = bf16[256,512]{1,0:T(8,128)(2,1)} copy(bf16[256,512]{1,0:T(8,128)(2,1)} %get-tuple-element.69) | data formatting | bytes 524288
Async XLA Ops:
  0.6 7.2 %copy-start.3 = (s32[16]{0:T(128)S(1)}, s32[16]{0:T(128)}, u32[]{:S(2)}) copy-start(s32[16]{0:T(128)} %prefix_ref.1) | copy-start | bytes 196
  0.6 7.2 %copy-start = (bf16[512,2048]{1,0:T(8,128)(2,1)S(1)}, bf16[512,2048]{1,0:T(8,128)(2,1)}, u32[]{:S(2)}) copy-start(bf16[512,2048]{1,0:T(8,128)(2,1)} %cache_ref.1) | copy-start | bytes 6291460
  0.7 7.2 %copy-start.1 = (bf16[256,256]{1,0:T(8,128)(2,1)S(1)}, bf16[256,256]{1,0:T(8,128)(2,1)}, u32[]{:S(2)}) copy-start(bf16[256,256]{1,0:T(8,128)(2,1)} %param.17) | copy-start | bytes 393220
  77.3 77.7 %copy-start.2 = (bf16[256,256]{1,0:T(8,128)(2,1)}, bf16[256,256]{1,0:T(8,128)(2,1)S(1)}, u32[]{:S(2)}) copy-start(bf16[256,256]{1,0:T(8,128)(2,1)S(1)} %get-tuple-element.66.attended_ref) | copy-start | bytes 393220

commit v3 on v2

v3 whole, which is shorter than its diff:
```python
import functools
import math

import jax
import jax.numpy as jnp
from jax import lax
from jax.experimental import pallas as pl
from jax.experimental.pallas import tpu as pltpu
from jax.sharding import PartitionSpec as P

HD = 256
PAGE = 16
TILE = 256
HALF = TILE // 2
MOST_PREFIX = 256
MESH = pl.DeviceIdType.MESH
VMEM_LIMIT = 60 * 1024 * 1024
FEW_PAGES = 7

masked_score = -1e30
lowest_peak = -1e20
norm_epsilon = 1e-05

START, LENGTH, SLOT, WHERE, SLOTS, COUNTS, MOST, TABLES = 0, 16, 32, 64, 320, 384, 448, 512

smem = pl.BlockSpec(memory_space=pltpu.SMEM)
vmem = pl.BlockSpec(memory_space=pltpu.VMEM)
hbm = pl.BlockSpec(memory_space=pl.ANY)


def shifted(value, size):
    return lax.shift_right_arithmetic(value, jnp.int32(size.bit_length() - 1))


def pack_kernel(
    shards,
    ids_ref,
    order_block_ref,
    prefix_ref,
    order_ref,
    fresh_ref,
    cache_ref,
    tiles,
    others,
    tables,
    tile_sem,
    page_sem,
):
    shard, group = lax.axis_index("tok"), lax.axis_index("grp")
    own_pages = order_ref.shape[0] // shards
    seg_count = prefix_ref.shape[0]
    side = group % 2
    pairs_at = (group // 2) * 2 * HD

    def columns(part):
        return pl.ds(pl.multiple_of(pairs_at + part * HD, HD), HD)

    def half_rows(which):
        return pl.ds(pl.multiple_of(which * HALF, HALF), HALF)

    fresh_copies = [
        pltpu.make_async_copy(
            fresh_ref.at[half_rows(side), columns(part)],
            tiles.at[part, pl.ds(0, HALF), :],
            tile_sem.at[part],
        )
        for part in range(2)
    ]
    fresh_copies.append(
        pltpu.make_async_copy(fresh_ref.at[half_rows(1 - side), columns(side)], others, tile_sem.at[2])
    )
    for copy in fresh_copies:
        copy.start()

    def page_copy(page, rank, part):
        return pltpu.make_async_copy(
            cache_ref.at[pl.ds(pl.multiple_of(page * PAGE, PAGE), PAGE), columns(part)],
            tiles.at[part, pl.ds(pl.multiple_of(HALF + rank * PAGE, PAGE), PAGE), :],
            page_sem.at[rank, part],
        )

    ids = ids_ref[...]
    starts = [jnp.int32(0)]
    for s in range(1, seg_count):
        starts.append(jnp.sum((ids < s).astype(jnp.float32)).astype(jnp.int32))
    starts.append(jnp.int32(ids_ref.shape[0] * ids_ref.shape[1]))
    slot = jnp.int32(0)
    for s in range(seg_count):
        length = starts[s + 1] - starts[s]
        tables[START + s] = starts[s]
        tables[LENGTH + s] = length
        tables[SLOT + s] = slot
        slot = slot + shifted(prefix_ref[s] + length + PAGE - 1, PAGE)
    tables[SLOT + seg_count] = slot

    for owner in range(2 * shards):
        tables[COUNTS + owner] = 0

    @pl.loop(0, seg_count)
    def _(s):
        first = tables[SLOT + s]

        @pl.loop(0, shifted(prefix_ref[s] + PAGE - 1, PAGE))
        def _(j):
            page = order_ref[first + j]
            owner = shifted(page, own_pages)
            parity = j & 1
            count = COUNTS + 2 * owner + parity
            rank = tables[count]
            tables[count] = rank + 1
            tables[WHERE + s * PAGE + j] = owner * own_pages + rank

            @pl.when((owner == shard) & (parity == side))
            def _():
                for part in range(2):
                    page_copy(page & (own_pages - 1), rank, part).start()

    most = jnp.int32(0)
    for owner in range(2 * shards):
        most = jnp.maximum(most, tables[COUNTS + owner])
    tables[MOST] = most

    order = order_block_ref[...]
    at = lax.broadcasted_iota(jnp.int32, order.shape, 0) * order.shape[1] + (
        lax.broadcasted_iota(jnp.int32, order.shape, 1)
    )
    at = at.astype(jnp.float32)
    for i in range(own_pages):
        mine = order == shard * own_pages + i
        tables[SLOTS + i] = jnp.sum(jnp.where(mine, at, 0.0)).astype(jnp.int32)

    @pl.loop(0, tables[COUNTS + 2 * shard + side])
    def _(rank):
        for part in range(2):
            page_copy(0, rank, part).wait()

    for copy in fresh_copies:
        copy.wait()


def pack(segment_ids, prefix_length, page_order, fresh, cache, shards):
    own_pages = page_order.shape[0] // shards
    return pl.pallas_call(
        functools.partial(pack_kernel, shards),
        out_shape=(
            jax.ShapeDtypeStruct((2, HALF + own_pages * PAGE, HD), jnp.bfloat16),
            jax.ShapeDtypeStruct((HALF, HD), jnp.bfloat16),
            jax.ShapeDtypeStruct((TABLES,), jnp.int32),
        ),
        in_specs=[vmem, vmem, smem, smem, hbm, hbm],
        out_specs=(vmem, vmem, smem),
        scratch_shapes=[
            pltpu.SemaphoreType.DMA((3,)),
            pltpu.SemaphoreType.DMA((own_pages, 2)),
        ],
        name="pack",
    )(
        segment_ids.reshape(-1, 128),
        page_order.reshape(-1, 128),
        prefix_length,
        page_order,
        fresh,
        cache,
    )


SIDE = 4
ROUTES = {
    (0, 0): ("p+", "p-", "q+", "q-", "core"),
    (3, 0): ("q+", "q-", "p+", "core"),
    (1, 0): ("q+", "q-", "core"),
    (0, 3): ("q+", "core"),
    (0, 1): ("core",),
    (2, 0): ("q+", "q-", "core"),
    (3, 3): ("q+", "core"),
    (3, 1): ("core",),
    (1, 3): ("core",),
    (1, 1): ("q-", "core"),
    (0, 2): ("core",),
    (2, 3): ("core",),
    (2, 1): ("q-", "core"),
    (3, 2): ("core",),
    (1, 2): ("core",),
    (2, 2): ("core",),
}
MOVES = {"p+": (1, 0), "p-": (-1, 0), "q+": (0, 1), "q-": (0, -1), "core": (0, 0)}
TILES = list(ROUTES)
MESSAGES = [(tile, way) for tile, ways in ROUTES.items() for way in ways]
Z_LAG = 3


def arrival(tile):
    for index, (sent, way) in enumerate(MESSAGES):
        move = MOVES[way]
        if way != "core" and ((sent[0] - move[0]) % SIDE, (sent[1] - move[1]) % SIDE) == tile:
            return index
    return None


def spread_kernel(
    rows,
    tiles_ref,
    others_ref,
    query_ref,
    pairs,
    rest,
    other_query,
    own,
    own_rest,
    send_sem,
    recv_sem,
    z_send,
    z_recv,
    core_send,
    core_recv,
    own_sem,
):
    shard, group = lax.axis_index("tok"), lax.axis_index("grp")
    side = group % 2
    partner = group + 1 - 2 * side
    core, x, y = shard % 2, (shard // 2) % SIDE, shard // (2 * SIDE)

    def shard_at(dx, dy, c):
        return (((y + dy + SIDE) % SIDE) * SIDE + (x + dx + SIDE) % SIDE) * 2 + c

    def place(part, p, q, c):
        return shard_at(p, q, c) if part == 0 else shard_at(q, p, c)

    def remote(source, target, send, recv, device):
        return pltpu.make_async_remote_copy(
            src_ref=source,
            dst_ref=target,
            send_sem=send,
            recv_sem=recv,
            device_id=device,
            device_id_type=MESH,
        )

    def message(part, index):
        tile, way = MESSAGES[index]
        move = MOVES[way]
        target = place(part, move[0], move[1], 1 - core if way == "core" else core)
        block = pairs.at[part, place(part, tile[0], tile[1], core)]
        source = tiles_ref.at[part, pl.ds(0, rows), :] if tile == (0, 0) else block
        sems = send_sem.at[part, index], recv_sem.at[part, index]
        return remote(source, block, *sems, {"tok": target})

    def z_message(n):
        p, q = TILES[n]
        there = shard_at(p * side + q * (1 - side), q * side + p * (1 - side), core)
        source = pairs.at[1 - side, there, pl.ds(0, HALF), :]
        return remote(source, rest.at[there], z_send.at[n], z_recv.at[n], {"grp": partner})

    def landing(n):
        p, q = TILES[n]
        return rest.at[shard_at(p * (1 - side) + q * side, q * (1 - side) + p * side, core)]

    def core_message(n):
        block = rest.at[shard] if n == 0 else landing(n)
        source = others_ref if n == 0 else block
        device = {"tok": shard_at(0, 0, 1 - core)}
        return remote(source, block, core_send.at[n], core_recv.at[n], device)

    query_message = remote(query_ref, other_query, z_send.at[0], z_recv.at[0], {"grp": partner})
    fetches = [
        pltpu.make_async_copy(tiles_ref.at[part, pl.ds(0, rows), :], own.at[part], own_sem.at[part])
        for part in range(2)
    ] + [pltpu.make_async_copy(others_ref, own_rest, own_sem.at[2])]
    stores = [
        pltpu.make_async_copy(own.at[part], pairs.at[part, shard], own_sem.at[part])
        for part in range(2)
    ] + [pltpu.make_async_copy(own_rest, rest.at[shard], own_sem.at[2])]

    barrier = pltpu.get_barrier_semaphore()
    peers = [shard_at(1, 0, core), shard_at(-1, 0, core), shard_at(0, 1, core)]
    peers += [shard_at(0, -1, core), shard_at(0, 0, 1 - core)]
    devices = [{"tok": peer} for peer in peers] + [{"grp": partner}]
    for device in devices:
        pl.semaphore_signal(barrier, inc=1, device_id=device, device_id_type=MESH)
    for fetch in fetches:
        fetch.start()
    pl.semaphore_wait(barrier, len(devices))

    def pass_rest(n):
        block = landing(n)
        remote(block, block, z_send.at[n], z_recv.at[n], {"grp": partner}).wait_recv()
        core_message(n).start()

    for n, tile in enumerate(TILES):
        sent = [i for i, (t, _) in enumerate(MESSAGES) if t == tile]
        for part in range(2):
            if n > 0:
                message(part, arrival(tile)).wait_recv()
            for i in sent:
                message(part, i).start()
        if n == 0:
            query_message.start()
            core_message(0).start()
        else:
            z_message(n).start()
        if n > Z_LAG:
            pass_rest(n - Z_LAG)
    for n in range(len(TILES) - Z_LAG, len(TILES)):
        pass_rest(n)
    for fetch, store in zip(fetches, stores):
        fetch.wait()
        store.start()
    for store in stores:
        store.wait()
    query_message.wait()
    for part in range(2):
        for i, (_, way) in enumerate(MESSAGES):
            if way == "core":
                message(part, i).wait_recv()
    for n in range(len(TILES)):
        core_message(n).wait_recv()
        core_message(n).wait_send()
        if n > 0:
            z_message(n).wait_send()
    for part in range(2):
        for i in range(len(MESSAGES)):
            message(part, i).wait_send()


def spread(tiles, others, queries, rows, shards, collective_id):
    many = pltpu.SemaphoreType.DMA((2, len(MESSAGES)))
    few = pltpu.SemaphoreType.DMA((len(TILES),))
    return pl.pallas_call(
        functools.partial(spread_kernel, rows),
        out_shape=(
            jax.ShapeDtypeStruct((2, shards, rows, HD), jnp.bfloat16),
            jax.ShapeDtypeStruct((shards, HALF, HD), jnp.bfloat16),
            jax.ShapeDtypeStruct(queries.shape, jnp.bfloat16),
        ),
        in_specs=[hbm] * 3,
        out_specs=(hbm, hbm, hbm),
        scratch_shapes=[
            pltpu.VMEM((2, rows, HD), jnp.bfloat16),
            pltpu.VMEM((HALF, HD), jnp.bfloat16),
            many,
            many,
            few,
            few,
            few,
            few,
            pltpu.SemaphoreType.DMA((3,)),
        ],
        compiler_params=pltpu.CompilerParams(collective_id=collective_id, has_side_effects=True),
        name="spread",
    )(tiles, others, queries)


STEP_TILES = 4
PAGE_STEP = 4


def attend_kernel(
    seg_count,
    tables,
    prefix_ref,
    q_ref,
    other_q_ref,
    pairs_ref,
    rest_ref,
    cache_ref,
    own_ref,
    other_ref,
    own_stats,
    other_stats,
    written_ref,
    tiles,
    prefix_tile,
    windows,
    query,
    peak,
    total,
    acc,
    place_seg,
    tile_sem,
    page_sem,
    window_sem,
    cache_sem,
):
    shard, group = lax.axis_index("tok"), lax.axis_index("grp")
    side = group % 2
    rows = q_ref.shape[0]
    own_pages = written_ref.shape[0] // PAGE
    shards = pairs_ref.shape[1]
    wide = STEP_TILES * HALF
    blocks = TILE // PAGE

    def cache_copy():
        columns = pl.ds(pl.multiple_of(group * HD, HD), HD)
        return pltpu.make_async_copy(cache_ref.at[:, columns], written_ref, cache_sem)

    def page_place(i, seg):
        position = (tables[SLOTS + i] - tables[SLOT + seg]) * PAGE
        return position, tables[START + seg] + position - prefix_ref[seg]

    def window_copy(source, i, which):
        return pltpu.make_async_copy(
            source, windows.at[i, pl.ds(which * PAGE, PAGE), :], window_sem.at[i, which]
        )

    def tile_copy(index, slot, n, part):
        return pltpu.make_async_copy(
            pairs_ref.at[part, jnp.maximum(index, 0), pl.ds(0, HALF), :],
            tiles.at[slot, part, pl.ds(n * HALF, HALF), :],
            tile_sem.at[slot, n, part],
        )

    def page_copy(seg, i, part):
        place = tables[WHERE + seg * PAGE + 2 * i + side]
        row = HALF + (place & (own_pages - 1)) * PAGE
        return pltpu.make_async_copy(
            pairs_ref.at[part, shifted(place, own_pages), pl.ds(pl.multiple_of(row, PAGE), PAGE), :],
            prefix_tile.at[part, pl.ds(pl.multiple_of(i * PAGE, PAGE), PAGE), :],
            page_sem.at[i, part],
        )

    first_row = shard * rows
    seg_lo = jnp.int32(-1)
    seg_hi = jnp.int32(-1)
    for s in range(seg_count):
        seg_lo = seg_lo + (tables[START + s] <= first_row).astype(jnp.int32)
        seg_hi = seg_hi + (tables[START + s] <= first_row + rows - 1).astype(jnp.int32)
    first_tile = shifted(tables[START + seg_lo], TILE)
    last_low = tables[START + seg_hi]
    steps = shifted(shard - first_tile, STEP_TILES) + 1
    base = shard + 1 - STEP_TILES * steps

    def start_tiles(step):
        for n in range(STEP_TILES):
            for part in range(2):
                tile_copy(base + STEP_TILES * step + n, step & 1, n, part).start()

    start_tiles(0)
    cache_copy().start()

    @pl.loop(0, own_pages)
    def _(i):
        slot = tables[SLOTS + i]
        seg = jnp.int32(-1)
        for s in range(seg_count):
            seg = seg + (tables[SLOT + s] <= slot).astype(jnp.int32)
        place_seg[i] = seg
        _, token = page_place(i, seg)
        first = shifted(token, PAGE)
        for which in range(2):
            block = jnp.clip(first + which, 0, shards * blocks - 1)
            tile, within = shifted(block, blocks), block & (blocks - 1)
            here = shifted(within, blocks // 2) == side
            row = pl.ds(pl.multiple_of((within & (blocks // 2 - 1)) * PAGE, PAGE), PAGE)

            @pl.when(here)
            def _():
                window_copy(pairs_ref.at[side, tile, row, :], i, which).start()

            @pl.when(jnp.logical_not(here))
            def _():
                window_copy(rest_ref.at[tile, row, :], i, which).start()

    prefix_tile[...] = jnp.zeros_like(prefix_tile)
    peak[...] = jnp.full_like(peak, lowest_peak)
    total[...] = jnp.zeros_like(total)
    acc[...] = jnp.zeros_like(acc)
    for n, source in enumerate((q_ref, other_q_ref)):
        query[pl.ds(n * rows, rows), :] = (
            source[...].astype(jnp.float32) * (1.0 / math.sqrt(HD))
        ).astype(jnp.bfloat16)
    row_at = first_row + (lax.broadcasted_iota(jnp.int32, (2 * rows, 1), 0) & (rows - 1))
    low = jnp.zeros((2 * rows, 1), jnp.int32)
    seg_at = jnp.full((2 * rows, 1), -1, jnp.int32)
    for s in range(seg_count):
        begun = row_at >= tables[START + s]
        low = jnp.where(begun, tables[START + s], low)
        seg_at = seg_at + begun.astype(jnp.int32)

    def absorb(keys, values, live):
        scores = lax.dot_general(
            query[...], keys, (((1,), (1,)), ((), ())), preferred_element_type=jnp.float32
        )
        if live is not None:
            scores = jnp.where(live, scores, masked_score)
        before = peak[...]
        raised = jnp.maximum(before, jnp.max(scores, axis=1, keepdims=True))
        weights = jnp.exp(scores - raised)
        rescale = jnp.exp(before - raised)
        peak[...] = raised
        total[...] = total[...] * rescale + jnp.sum(weights, axis=1, keepdims=True)
        acc[...] = acc[...] * rescale + jnp.dot(
            weights.astype(jnp.bfloat16), values, preferred_element_type=jnp.float32
        )

    @pl.loop(0, steps)
    def _(step):
        slot = step & 1
        for n in range(STEP_TILES):
            for part in range(2):
                tile_copy(base + STEP_TILES * step + n, slot, n, part).wait()

        @pl.when(step + 1 < steps)
        def _():
            start_tiles(step + 1)

        at = (base + STEP_TILES * step) * TILE
        whole = (at >= last_low) & (step + 1 < steps)

        @pl.when(whole)
        def _():
            absorb(tiles[slot, 0], tiles[slot, 1], None)

        @pl.when(jnp.logical_not(whole))
        def _():
            column = lax.broadcasted_iota(jnp.int32, (1, wide), 1)
            key_at = at + shifted(column, HALF) * TILE + side * HALF + (column & (HALF - 1))
            absorb(tiles[slot, 0], tiles[slot, 1], (key_at >= low) & (key_at <= row_at))

    @pl.loop(seg_lo, seg_hi + 1)
    def _(seg):
        pages = shifted(prefix_ref[seg] + PAGE - 1, PAGE)
        count = shifted(pages + 1 - side, 2)

        @pl.loop(0, count)
        def _(i):
            for part in range(2):
                page_copy(seg, i, part).start()

        @pl.loop(0, count)
        def _(i):
            for part in range(2):
                page_copy(seg, i, part).wait()

        @pl.when(count > 0)
        def _():
            column = lax.broadcasted_iota(jnp.int32, (1, prefix_tile.shape[1]), 1)
            at = (2 * shifted(column, PAGE) + side) * PAGE + (column & (PAGE - 1))
            absorb(prefix_tile[0], prefix_tile[1], (seg_at == seg) & (at < prefix_ref[seg]))

    summed = total[...]
    part = acc[...] / jnp.where(summed > 0.0, summed, 1.0)
    own_ref[...] = part[:rows]
    other_ref[...] = part[rows:].astype(jnp.bfloat16)
    line = lax.broadcasted_iota(jnp.int32, (128, 128), 0)
    diagonal = line == lax.broadcasted_iota(jnp.int32, (128, 128), 1)
    for n, stats in enumerate((own_stats, other_stats)):
        stats[...] = jnp.zeros_like(stats)
        for m, column in enumerate((peak, total)):
            for r in range(rows // 128):
                values = column[pl.ds(n * rows + r * 128, 128), :]
                spread_out = jnp.where(diagonal, values, 0.0)
                stats[pl.ds(m * (rows // 128) + r, 1), :] = jnp.sum(
                    spread_out, axis=0, keepdims=True
                )

    cache_copy().wait()

    @pl.loop(0, own_pages // PAGE_STEP)
    def _(group_of_pages):
        for n in range(PAGE_STEP):
            i = group_of_pages * PAGE_STEP + n
            seg = place_seg[i]
            position, token = page_place(i, seg)
            for which in range(2):
                window_copy(rest_ref.at[0, pl.ds(0, PAGE), :], i, which).wait()
            shift = token & (PAGE - 1)
            to = lax.broadcasted_iota(jnp.int32, (PAGE, 2 * PAGE), 0)
            taken = lax.broadcasted_iota(jnp.int32, (PAGE, 2 * PAGE), 1)
            picked = (taken == to + shift).astype(jnp.bfloat16)
            fresh = jnp.dot(picked, windows[i], preferred_element_type=jnp.float32)
            at = position + lax.broadcasted_iota(jnp.int32, (PAGE, HD), 0)
            used = tables[SLOTS + i] < tables[SLOT + seg_count]
            until = jnp.where(used, prefix_ref[seg] + tables[LENGTH + seg], 0)
            live = (at >= prefix_ref[seg]) & (at < until)
            block = pl.ds(pl.multiple_of(i * PAGE, PAGE), PAGE)
            held = written_ref[block, :].astype(jnp.float32)
            written_ref[block, :] = jnp.where(live, fresh, held).astype(jnp.bfloat16)


def attend(tables, prefix_length, queries, other_queries, pairs, rest, cache):
    rows = queries.shape[0]
    most = MOST_PREFIX // 2
    own_pages = cache.shape[0] // PAGE
    stats = jax.ShapeDtypeStruct((8, 128), jnp.float32)
    return pl.pallas_call(
        functools.partial(attend_kernel, prefix_length.shape[0]),
        out_shape=(
            jax.ShapeDtypeStruct((rows, HD), jnp.float32),
            jax.ShapeDtypeStruct((rows, HD), jnp.bfloat16),
            stats,
            stats,
            jax.ShapeDtypeStruct((cache.shape[0], HD), jnp.bfloat16),
        ),
        in_specs=[smem, smem, vmem, vmem, hbm, hbm, hbm],
        out_specs=(vmem,) * 5,
        scratch_shapes=[
            pltpu.VMEM((2, 2, STEP_TILES * HALF, HD), jnp.bfloat16),
            pltpu.VMEM((2, most, HD), jnp.bfloat16),
            pltpu.VMEM((own_pages, 2 * PAGE, HD), jnp.bfloat16),
            pltpu.VMEM((2 * rows, HD), jnp.bfloat16),
            pltpu.VMEM((2 * rows, 1), jnp.float32),
            pltpu.VMEM((2 * rows, 1), jnp.float32),
            pltpu.VMEM((2 * rows, HD), jnp.float32),
            pltpu.SMEM((own_pages,), jnp.int32),
            pltpu.SemaphoreType.DMA((2, STEP_TILES, 2)),
            pltpu.SemaphoreType.DMA((most // PAGE, 2)),
            pltpu.SemaphoreType.DMA((own_pages, 2)),
            pltpu.SemaphoreType.DMA(()),
        ],
        name="attend",
    )(tables, prefix_length, queries, other_queries, pairs, rest, cache)


def chain_kernel(
    groups,
    own_ref,
    other_ref,
    own_stats,
    other_stats,
    residual_ref,
    post_gain_ref,
    next_gain_ref,
    wo_hbm,
    wg_hbm,
    wu_hbm,
    wd_hbm,
    wn_hbm,
    attended_ref,
    layer_ref,
    next_ref,
    part_in,
    stats_in,
    wo,
    wg,
    wu,
    wd,
    wn,
    partial,
    hidden,
    sums,
    outgoing,
    incoming,
    gathered,
    weight_sem,
    part_send,
    part_recv,
    sum_send,
    sum_recv,
    copy_send,
    copy_recv,
):
    me = lax.axis_index("grp")
    width = layer_ref.shape[1]
    chunk = layer_ref.shape[0]
    half = width // 2
    far = groups // 2
    steps = (1, -1)
    neighbour = [lax.rem(me + 1, groups), lax.rem(me + groups - 1, groups)]

    loads = []
    for i, (source, target) in enumerate(
        ((wo_hbm, wo), (wg_hbm, wg), (wu_hbm, wu), (wd_hbm, wd), (wn_hbm, wn))
    ):
        loads.append(pltpu.make_async_copy(source, target, weight_sem.at[i]))
        loads[i].start()

    barrier = pltpu.get_barrier_semaphore()
    for d in range(2):
        pl.semaphore_signal(
            barrier, inc=1, device_id={"grp": neighbour[d]}, device_id_type=MESH
        )
    pl.semaphore_wait(barrier, 2)

    swaps = [
        pltpu.make_async_remote_copy(
            src_ref=source,
            dst_ref=target,
            send_sem=part_send.at[i],
            recv_sem=part_recv.at[i],
            device_id={"grp": me + 1 - 2 * (me % 2)},
            device_id_type=MESH,
        )
        for i, (source, target) in enumerate(((other_stats, stats_in), (other_ref, part_in)))
    ]
    for swap in swaps:
        swap.start()

    def rows_of(owner):
        index = lax.rem(owner + 2 * groups, groups)
        return pl.ds(pl.multiple_of(index * chunk, chunk), chunk)

    def columns_of(h):
        return pl.ds(h * half, half)

    def sum_copy(phase, d, h, s):
        return pltpu.make_async_remote_copy(
            src_ref=outgoing.at[phase, d, h, s],
            dst_ref=incoming.at[phase, d, h, s],
            send_sem=sum_send.at[phase, d, h, s],
            recv_sem=sum_recv.at[phase, d, h, s],
            device_id={"grp": neighbour[d]},
            device_id_type=MESH,
        )

    def gather_copy(phase, d, h, k):
        block = gathered.at[phase, rows_of(me - steps[d] * k), columns_of(h)]
        return pltpu.make_async_remote_copy(
            src_ref=block,
            dst_ref=block,
            send_sem=copy_send.at[phase, d, h, k],
            recv_sem=copy_recv.at[phase, d, h, k],
            device_id={"grp": neighbour[d]},
            device_id_type=MESH,
        )

    def reduce_scatter(phase):
        for s in range(far):
            for h in range(2):
                for d in range(2):
                    first = 0 if h == d else 1
                    if s < first:
                        continue
                    owner = me + steps[d] * (far - s)
                    value = partial[rows_of(owner), columns_of(h)]
                    if s > first:
                        sum_copy(phase, d, h, s - 1).wait_recv()
                        value = value + incoming[phase, d, h, s - 1].astype(jnp.float32)
                    outgoing[phase, d, h, s] = value.astype(jnp.bfloat16)
                    sum_copy(phase, d, h, s).start()
        for h in range(2):
            value = partial[rows_of(me), columns_of(h)]
            for d in range(2):
                sum_copy(phase, d, h, far - 1).wait_recv()
                value = value + incoming[phase, d, h, far - 1].astype(jnp.float32)
            sums[:, columns_of(h)] = value
        for s in range(far):
            for h in range(2):
                for d in range(2):
                    if s >= (0 if h == d else 1):
                        sum_copy(phase, d, h, s).wait_send()

    def all_gather(phase):
        for k in range(far):
            for h in range(2):
                for d in range(2):
                    if k >= (far if h == d else far - 1):
                        continue
                    if k > 0:
                        gather_copy(phase, d, h, k - 1).wait_recv()
                    gather_copy(phase, d, h, k).start()
        for h in range(2):
            for d in range(2):
                gather_copy(phase, d, h, (far if h == d else far - 1) - 1).wait_recv()
        for k in range(far):
            for h in range(2):
                for d in range(2):
                    if k < (far if h == d else far - 1):
                        gather_copy(phase, d, h, k).wait_send()

    def normed(values, gain_ref):
        scaled = values * lax.rsqrt(
            jnp.mean(values * values, axis=-1, keepdims=True) + norm_epsilon
        )
        return (scaled * gain_ref[...]).astype(jnp.bfloat16)

    rows = attended_ref.shape[0]
    line = lax.broadcasted_iota(jnp.int32, (128, 128), 0)
    diagonal = line == lax.broadcasted_iota(jnp.int32, (128, 128), 1)

    def column_of(stats, row):
        values = jnp.broadcast_to(stats[pl.ds(row, 1), :], (128, 128))
        return jnp.sum(jnp.where(diagonal, values, 0.0), axis=1, keepdims=True)

    for swap in swaps:
        swap.wait_recv()
    blocks = rows // 128
    for r in range(blocks):
        peaks = [column_of(stats, r) for stats in (own_stats, stats_in)]
        totals = [column_of(stats, blocks + r) for stats in (own_stats, stats_in)]
        highest = jnp.maximum(peaks[0], peaks[1])
        shares = [t * jnp.exp(p - highest) for p, t in zip(peaks, totals)]
        block = pl.ds(r * 128, 128)
        merged = own_ref[block, :] * shares[0] + part_in[block, :].astype(jnp.float32) * shares[1]
        attended_ref[block, :] = (merged / (shares[0] + shares[1])).astype(jnp.bfloat16)
    for swap in swaps:
        swap.wait_send()

    loads[0].wait()

    @pl.loop(0, width // 256)
    def _(j):
        columns = pl.ds(pl.multiple_of(j * 256, 256), 256)
        partial[:, columns] = jnp.dot(
            attended_ref[...], wo[:, columns], preferred_element_type=jnp.float32
        )

    reduce_scatter(0)
    first_sum = (residual_ref[...].astype(jnp.float32) + sums[...]).astype(jnp.bfloat16)
    layer_ref[...] = first_sum
    gathered[0, rows_of(me), :] = normed(first_sum.astype(jnp.float32), post_gain_ref)
    all_gather(0)

    loads[1].wait()
    loads[2].wait()

    @pl.loop(0, wg.shape[1] // 256)
    def _(j):
        columns = pl.ds(pl.multiple_of(j * 256, 256), 256)
        rows = gathered[0]
        gate = jnp.dot(rows, wg[:, columns], preferred_element_type=jnp.float32)
        up = jnp.dot(rows, wu[:, columns], preferred_element_type=jnp.float32)
        hidden[:, columns] = (jax.nn.silu(gate) * up).astype(jnp.bfloat16)

    loads[3].wait()

    @pl.loop(0, width // 256)
    def _(j):
        columns = pl.ds(pl.multiple_of(j * 256, 256), 256)
        partial[:, columns] = jnp.dot(
            hidden[...], wd[:, columns], preferred_element_type=jnp.float32
        )

    reduce_scatter(1)
    layer_out = (layer_ref[...].astype(jnp.float32) + sums[...]).astype(jnp.bfloat16)
    layer_ref[...] = layer_out
    gathered[1, rows_of(me), :] = normed(layer_out.astype(jnp.float32), next_gain_ref)
    all_gather(1)

    loads[4].wait()

    @pl.loop(0, wn.shape[1] // 256)
    def _(j):
        columns = pl.ds(pl.multiple_of(j * 256, 256), 256)
        next_ref[:, columns] = jnp.dot(
            gathered[1], wn[:, columns], preferred_element_type=jnp.float32
        ).astype(jnp.bfloat16)


def chain(parts, residual, post_gain, next_gain, wo, wg, wu, wd, wn, groups):
    rows = parts[0].shape[0]
    chunk, width = residual.shape
    far = groups // 2
    messages = (2, 2, 2, far)
    return pl.pallas_call(
        functools.partial(chain_kernel, groups),
        out_shape=(
            jax.ShapeDtypeStruct((rows, HD), jnp.bfloat16),
            jax.ShapeDtypeStruct((chunk, width), jnp.bfloat16),
            jax.ShapeDtypeStruct((rows, wn.shape[1]), jnp.bfloat16),
        ),
        in_specs=[vmem] * 7 + [hbm] * 5,
        out_specs=(vmem, vmem, vmem),
        scratch_shapes=[
            pltpu.VMEM((rows, HD), jnp.bfloat16),
            pltpu.VMEM((8, 128), jnp.float32),
        ]
        + [pltpu.VMEM(w.shape, w.dtype) for w in (wo, wg, wu, wd, wn)]
        + [
            pltpu.VMEM((rows, width), jnp.float32),
            pltpu.VMEM((rows, wg.shape[1]), jnp.bfloat16),
            pltpu.VMEM((chunk, width), jnp.float32),
            pltpu.VMEM(messages + (chunk, width // 2), jnp.bfloat16),
            pltpu.VMEM(messages + (chunk, width // 2), jnp.bfloat16),
            pltpu.VMEM((2, rows, width), jnp.bfloat16),
            pltpu.SemaphoreType.DMA((5,)),
            pltpu.SemaphoreType.DMA((2,)),
            pltpu.SemaphoreType.DMA((2,)),
            pltpu.SemaphoreType.DMA(messages),
            pltpu.SemaphoreType.DMA(messages),
            pltpu.SemaphoreType.DMA(messages),
            pltpu.SemaphoreType.DMA(messages),
        ],
        compiler_params=pltpu.CompilerParams(
            collective_id=1, has_side_effects=True, vmem_limit_bytes=VMEM_LIMIT
        ),
        name="chain",
    )(*parts, residual, post_gain, next_gain, wo, wg, wu, wd, wn)


def copy_kernel(*refs):
    count = len(refs) // 2
    for source, target in zip(refs[:count], refs[count:]):
        target[...] = source[...]


def local(
    residual_in,
    queries,
    fresh_pairs,
    cache_pairs,
    segment_ids,
    prefix_length,
    page_order,
    out_weight,
    post_gain,
    gate_weight,
    up_weight,
    down_weight,
    next_gain,
    next_weight,
):
    groups, shards = lax.axis_size("grp"), lax.axis_size("tok")
    own_pages = page_order.shape[0] // shards
    tiles, others, tables = pack(
        segment_ids, prefix_length, page_order, fresh_pairs, cache_pairs, shards
    )

    def attention(pages, collective_id):
        rows = HALF + pages * PAGE
        pairs, rest, other_queries = spread(tiles, others, queries, rows, shards, collective_id)
        return attend(tables, prefix_length, queries, other_queries, pairs, rest, cache_pairs)

    *parts, written = lax.cond(
        tables[MOST] <= FEW_PAGES,
        lambda: attention(FEW_PAGES, 2),
        lambda: attention(own_pages, 3),
    )
    results = chain(
        (parts[0], parts[1], parts[2], parts[3]),
        residual_in,
        post_gain[None, :],
        next_gain[None, :],
        out_weight,
        gate_weight,
        up_weight,
        down_weight,
        next_weight,
        groups,
    )
    attended, layer_out, next_proj = pl.pallas_call(
        copy_kernel,
        out_shape=tuple(jax.ShapeDtypeStruct(a.shape, a.dtype) for a in results),
        in_specs=[vmem] * 3,
        out_specs=(vmem,) * 3,
        name="results",
    )(*results)
    return (attended, written, layer_out, next_proj)


def solution(mesh):
    in_specs = (
        P(("tok", "grp"), None),
        P("tok", "grp"),
        P("tok", None),
        P("tok", None),
        P(),
        P(),
        P(),
        P("grp", None),
        P(),
        P(None, "grp"),
        P(None, "grp"),
        P("grp", None),
        P(),
        P(None, "grp"),
    )
    out_specs = (P("tok", "grp"), P("tok", "grp"), P(("tok", "grp"), None), P("tok", "grp"))
    return jax.shard_map(local, mesh=mesh, in_specs=in_specs, out_specs=out_specs, check_vma=False)
```

time: 159 us -> 146 us (0.918)
  Pallas kernels: 153 us -> 142 us
  local copies, waits for them, and re-layouts: 3.84 us -> 0.59 us
    pallas_call x2 -> x3, Pallas kernels: 53.7 us -> 41.9 us  [the longest x1 35.4 us: spread(): pl.pallas_call(functools.partial(spread_kernel, rows), out_shape=(jax.Sha...]
    pallas_call x1, Pallas kernels: 77.7 us -> 81.6 us  [chain(): pl.pallas_call(functools.partial(chain_kernel, groups), out_shape=(jax.Sh...]
    pallas_call x1, Pallas kernels: 21.7 us -> 18.4 us  [attend(): pl.pallas_call(functools.partial(attend_kernel, prefix_length.shape[0]),...]
    unnamed x10 -> x6, local copies, waits for them, and re-layouts: 3.26 us -> 0.01 us
where the time goes in v3:
time: 146 us; the launch traced here: 144 us
  Pallas kernels  142 us (97%)
    pallas_call x1, Pallas kernels, chain(): pl.pallas_call(functools.partial(chain_kernel, groups), out_shape=(jax.Sh...  81.6 us
    pallas_call x1, Pallas kernels, spread(): pl.pallas_call(functools.partial(spread_kernel, rows), out_shape=(jax.Sha...  35.4 us
    pallas_call x1, Pallas kernels, attend(): pl.pallas_call(functools.partial(attend_kernel, prefix_length.shape[0]),...  18.4 us
    pallas_call x1, Pallas kernels, pack(): pl.pallas_call(functools.partial(pack_kernel, shards), out_shape=(jax.Sha...  4.65 us

profile of v3, /device:TPU:30, one launch (start us, length us, event | category | flops | bytes accessed | tf_op | source)
XLA Modules:
  0.0 144.1 jit_solution(16542343992132044419)
XLA Ops:
  0.6 0.0 copy-start.2
  0.6 0.0 copy-start
  0.7 0.0 copy-start.1
  0.7 4.7 %pack.1 = (bf16[2,640,256]{2,1,0:T(8,128)(2,1)S(1)}, bf16[128,256]{1,0:T(8,128)(2,1)S(1)}, s32[512]{0:T(512)S(1)}) custom-call(s32[64,128]{1,0:T(8,128)} %bitcast.5, s32[8,128]{1,0:T(8,128)} %bitcast.6, s32[16]{0:T(128)} %prefix_ref.1, s32[1024]{0:T(1024)} %order_ref.1, bf16[256,2048]{1,0:T(8,128)(2,1)} %fresh_ref.1, bf16[512,2048]{1,0:T(8,128)(2,1)} %cache_ref.1), custom_call_target="tpu_custom_call" | custom-call | tf_op jit(solution)/shard_map/pack/pallas_call | solution.py:143
  5.3 0.6 slice.3
  6.6 0.0 copy-done.2
  6.6 0.0 copy-done
  6.6 0.0 copy-done.1
  6.6 53.9 %conditional.1 = ((f32[256,256]{1,0:T(8,128)S(1)}, bf16[256,256]{1,0:T(8,128)(2,1)S(1)}, f32[8,128]{1,0:T(8,128)S(1)}, f32[8,128]{1,0:T(8,128)S(1)}, bf16[512,256]{1,0:T(8,128)(2,1)})) conditional(s32[]{:T(128)} %bitcast.2, (bf16[2,640,256]{2,1,0:T(8,128)(2,1)S(1)}, bf16[128,256]{1,0:T(8,128)(2,1)S(1)}, bf16[256,256]{1,0:T(8,128)(2,1)S(1)}, ...), branch_computations={%region_0.0_spmd, %region_1.0_spmd} | conditional | bytes 8 | solution.py:913
  6.6 35.4 %spread.3 = (bf16[2,32,240,256]{3,2,1,0:T(8,128)(2,1)}, bf16[32,128,256]{2,1,0:T(8,128)(2,1)}, bf16[256,256]{1,0:T(8,128)(2,1)}) custom-call(bf16[2,640,256]{2,1,0:T(8,128)(2,1)S(1)} %get-tuple-element.36.tiles_ref, bf16[128,256]{1,0:T(8,128)(2,1)S(1)} %get-tuple-element.37.others_ref, bf16[256,256]{1,0:T(8,128)(2,1)S(1)} %get-tuple-element.35.query_ref.q_ref), custom_call_target="tpu_custom_call" | custom-call | tf_op jit(solution)/shard_map/cond/branch_1_fun/spread/pallas_call | solution.py:328
  42.0 18.4 %attend.3 = (f32[256,256]{1,0:T(8,128)S(1)}, bf16[256,256]{1,0:T(8,128)(2,1)S(1)}, f32[8,128]{1,0:T(8,128)S(1)}, f32[8,128]{1,0:T(8,128)S(1)}, bf16[512,256]{1,0:T(8,128)(2,1)}) custom-call(s32[512]{0:T(512)S(1)} %get-tuple-element.33.tables, s32[16]{0:T(128)S(1)} %get-tuple-element.34.prefix_ref, bf16[256,256]{1,0:T(8,128)(2,1)S(1)} %get-tuple-element.35.query_ref.q_ref, ...), custom_call_target="tpu_custom_call" | custom-call | tf_op jit(solution)/shard_map/cond/branch_1_fun/attend/pallas_call | solution.py:585
  60.5 81.6 %chain.1 = (bf16[256,256]{1,0:T(8,128)(2,1)}, bf16[32,2048]{1,0:T(8,128)(2,1)}, bf16[256,512]{1,0:T(8,128)(2,1)}) custom-call(f32[256,256]{1,0:T(8,128)S(1)} %get-tuple-element.63.own_ref, bf16[256,256]{1,0:T(8,128)(2,1)S(1)} %get-tuple-element.64.other_ref, f32[8,128]{1,0:T(8,128)S(1)} %get-tuple-element.65.own_stats, ...), custom_call_target="tpu_custom_call" | custom-call | tf_op jit(solution)/shard_map/chain/pallas_call | solution.py:844
  142.2 1.9 %results.1 = (bf16[256,256]{1,0:T(8,128)(2,1)}, bf16[32,2048]{1,0:T(8,128)(2,1)}, bf16[256,512]{1,0:T(8,128)(2,1)}) custom-call(bf16[256,256]{1,0:T(8,128)(2,1)} %get-tuple-element.67.refs_0_, bf16[32,2048]{1,0:T(8,128)(2,1)} %get-tuple-element.68.refs_1_, bf16[256,512]{1,0:T(8,128)(2,1)} %get-tuple-element.69.refs_2_), custom_call_target="tpu_custom_call" | custom-call | tf_op jit(solution)/shard_map/results/pallas_call | solution.py:930
Async XLA Ops:
  0.6 5.9 %copy-start.2 = (s32[16]{0:T(128)S(1)}, s32[16]{0:T(128)}, u32[]{:S(2)}) copy-start(s32[16]{0:T(128)} %prefix_ref.1) | copy-start | bytes 196
  0.6 5.9 %copy-start = (bf16[512,2048]{1,0:T(8,128)(2,1)S(1)}, bf16[512,2048]{1,0:T(8,128)(2,1)}, u32[]{:S(2)}) copy-start(bf16[512,2048]{1,0:T(8,128)(2,1)} %cache_ref.1) | copy-start | bytes 6291460
  0.7 5.9 %copy-start.1 = (bf16[256,256]{1,0:T(8,128)(2,1)S(1)}, bf16[256,256]{1,0:T(8,128)(2,1)}, u32[]{:S(2)}) copy-start(bf16[256,256]{1,0:T(8,128)(2,1)} %param.17) | copy-start | bytes 393220
